TPU v7x, 32 devices: a whole 2x2x4 slice. The times are simulated.
32 devices in a mesh: tile: 8 (over y, x, core), mem: 4 (over z).
Axes of the slice: x: 2, y: 2, z: 4, core: 2. Of those that a mesh axis runs over, the one named last changes fastest.
Arguments:
- velocity: bfloat16 [96, 2, 8, 32768], P('mem', None, None, 'tile'), may hold values from -6 to 6
- start_frac: float32 [2, 16384], P(None, 'tile'), may hold values from 0 to 1
- observed: float32 [2, 16384], P(None, 'tile'), may hold values from -0.5 to 1.5
- obs_sd: float32 [16384], P('tile'), may hold values from 0.3 to 3
- tile_of: int32 [16384, 1], P('tile'), may hold values from 0 to 7; in each aligned block of 2048 rows (0 to 2047, 2048 to 4095, ...) at most 512 rows name the same one
- cell_of: int32 [16384], P('tile'), may hold values from 0 to 4030, as said below
Outputs:
- analysis_velocity: bfloat16 [96, 2, 8, 32768], P('mem', None, None, 'tile')
- analysis_positions: float32 [96, 2, 16384], P('mem', None, 'tile')
Inputs may be any that keep to these rules, and one draw needn't show every extreme that they name: cell_of is i * 64 + j with i and j below 63, so the stencil's four cells lie in the same tile. `tile_of`: of the drifters of one index of tile, at most 512 name one tile, a bound that some block reaches of them.
All inputs are finite; a program needn't handle non-finite values.
Results may differ from a plain program's by a relative error of at most 0.0048.
Values may be sent and summed in bfloat16 or wider, within the bound.
No kernel may reach another device: no remote copies, remote signals or barrier semaphores. Data moves between devices by JAX's collectives and lax.ppermute only.
A program may use at most 64 MiB of HBM per device.

v0:
```python
import functools
import math

import jax
import jax.numpy as jnp
from jax import lax
from jax.experimental import pallas as pl
from jax.experimental.pallas import tpu as pltpu
from jax.sharding import PartitionSpec as P

BX = 64
LANES = 128
STEP = 0.2
BF16 = jnp.bfloat16
F32 = jnp.float32
I32 = jnp.int32
HIGHEST = lax.Precision.HIGHEST
NT = (((1,), (1,)), ((), ()))


def iota(shape, dim):
    return lax.broadcasted_iota(I32, shape, dim)


def quotient(values, divisor):
    return ((values.astype(F32) + 0.5) * (1.0 / divisor)).astype(I32)


def ones_where(mask, dtype=BF16):
    return jnp.where(mask, 1.0, 0.0).astype(dtype)


def vmem():
    return pl.BlockSpec(memory_space=pltpu.VMEM)


def pack_kernel(local, levels, share, v_ref, halo_ref, zero_ref, rest0_ref, rest1_ref):
    rows = v_ref.shape[0]
    i = iota((2 * local, rows), 0)
    j = iota((2 * local, rows), 1)
    comp = (i >= local).astype(I32)
    pick = ones_where(j == ((i - comp * local) * 2 + comp) * levels)
    x = v_ref[...]
    zero_ref[0, :, :share] = jnp.dot(pick, x, preferred_element_type=F32).astype(BF16)
    zero_ref[0, :, share:] = jnp.dot(pick, halo_ref[...], preferred_element_type=F32).astype(BF16)
    other = levels - 1
    i = iota((other * local, rows), 0)
    j = iota((other * local, rows), 1)
    member = quotient(i, other)
    base = member * 2 * levels + (i - member * other) + 1
    for c, ref in enumerate((rest0_ref, rest1_ref)):
        pick = ones_where(j == base + c * levels)
        ref[0] = jnp.dot(pick, x, preferred_element_type=F32).astype(BF16)


def pack(velocity, shares):
    local, _, levels, cells = velocity.shape
    share = cells // shares
    rows = local * 2 * levels
    flat = velocity.reshape(rows, cells)
    steps = share // LANES
    last = cells // LANES - 1
    other = (levels - 1) * local
    return pl.pallas_call(
        functools.partial(pack_kernel, local, levels, share),
        grid=(shares,),
        in_specs=[
            pl.BlockSpec((rows, share), lambda q: (0, q)),
            pl.BlockSpec((rows, LANES), lambda q: (0, jnp.minimum((q + 1) * steps, last))),
        ],
        out_specs=[
            pl.BlockSpec((1, 2 * local, share + LANES), lambda q: (q, 0, 0)),
            pl.BlockSpec((1, other, share), lambda q: (q, 0, 0)),
            pl.BlockSpec((1, other, share), lambda q: (q, 0, 0)),
        ],
        out_shape=[
            jax.ShapeDtypeStruct((shares, 2 * local, share + LANES), BF16),
            jax.ShapeDtypeStruct((shares, other, share), BF16),
            jax.ShapeDtypeStruct((shares, other, share), BF16),
        ],
        name="pack",
    )(flat, flat)


def route_kernel(tiles, blocks, share, q_ref, tile_ref, cell_ref, frac_ref, obs_ref, sd_ref, req_ref, where_ref, count_ref):
    drifters = cell_ref.shape[1]
    dest = tile_ref[...]
    local_cell = cell_ref[...] - q_ref[0] * share
    mine = jnp.logical_and(local_cell >= 0, local_cell < share)
    named = jnp.where(jnp.logical_and(iota((tiles, drifters), 0) == dest, mine), 1.0, 0.0)
    upper = ones_where(iota((LANES, LANES), 0) <= iota((LANES, LANES), 1))
    before = jnp.zeros((tiles, 1), F32)
    sums = []
    for start in range(0, drifters, LANES):
        part = named[:, start : start + LANES]
        sums.append(jnp.dot(part.astype(BF16), upper, preferred_element_type=F32) + before)
        before = before + jnp.sum(part, axis=1, keepdims=True)
    running = jnp.concatenate(sums, axis=1)
    slot = jnp.sum(named * (running - 1.0), axis=0, keepdims=True).astype(I32)
    total = jnp.sum(named * before, axis=0, keepdims=True)
    where_to = jnp.where(mine, dest * (blocks * LANES) + slot, -1)
    where_ref[...] = where_to
    count_ref[...] = jnp.broadcast_to(before, count_ref.shape)
    payload = jnp.concatenate(
        [local_cell.astype(F32), frac_ref[...], obs_ref[...], sd_ref[...], jnp.ones_like(total), total], axis=0
    )
    high = lax.shift_right_arithmetic(where_to, int(math.log2(LANES)))
    low = jnp.bitwise_and(where_to, LANES - 1)
    spread = jnp.concatenate([jnp.where(high == h, payload, 0.0) for h in range(tiles * blocks)], axis=0)
    place = ones_where(iota((LANES, drifters), 0) == low, F32)
    placed = lax.dot_general(spread, place, NT, precision=HIGHEST, preferred_element_type=F32)
    per = 8 * blocks
    for t in range(tiles):
        req_ref[t] = placed[t * per : (t + 1) * per]


def route(q, tile_of, cell_of, start_frac, observed, obs_sd, tiles, blocks, share):
    drifters = cell_of.shape[0]
    return pl.pallas_call(
        functools.partial(route_kernel, tiles, blocks, share),
        in_specs=[pl.BlockSpec(memory_space=pltpu.SMEM)] + [vmem()] * 5,
        out_specs=[vmem()] * 3,
        out_shape=[
            jax.ShapeDtypeStruct((tiles, 8 * blocks, LANES), F32),
            jax.ShapeDtypeStruct((1, drifters), I32),
            jax.ShapeDtypeStruct((tiles, LANES), F32),
        ],
        name="route",
    )(
        q.reshape(1),
        tile_of.reshape(1, drifters),
        cell_of.reshape(1, drifters),
        start_frac,
        observed,
        obs_sd.reshape(1, drifters),
    )


def bilinear(corner, x, y):
    return (1.0 - x) * (1.0 - y) * corner[0] + x * (1.0 - y) * corner[1] + (1.0 - x) * y * corner[2] + x * y * corner[3]


def block_count(value):
    return lax.shift_right_arithmetic(jnp.max(value).astype(I32) + (LANES - 1), int(math.log2(LANES)))


def observe_kernel(members, local, zero_ref, req_ref, pred_ref, gram_ref, table_ref, corner_ref):
    sources = req_ref.shape[0]
    rows, width = zero_ref.shape
    i = iota((rows, rows), 0)
    j = iota((rows, rows), 1)
    comp = (i >= members).astype(I32)
    member = i - comp * members
    source = quotient(member, local)
    pick = ones_where(j == source * 2 * local + comp * local + member - source * local)
    table = jnp.dot(pick, zero_ref[...], preferred_element_type=F32)
    for n, offset in enumerate((0, 1, BX, BX + 1)):
        moved = table if offset == 0 else pltpu.roll(table, width - offset, 1)
        table_ref[n * rows : (n + 1) * rows, :] = moved.astype(BF16)
    gram_ref[...] = jnp.zeros_like(gram_ref)
    spread = math.sqrt(members - 1)

    def one_block(s, b):
        r = req_ref[s, pl.ds(pl.multiple_of(b * 8, 8), 8), :]
        cell = r[0:1].astype(I32)
        hit = ones_where(iota((width, LANES), 0) == cell)
        corner_ref[...] = jnp.dot(table_ref[...], hit, preferred_element_type=F32)
        cx = [corner_ref[n * rows : n * rows + members, :] for n in range(4)]
        cy = [corner_ref[n * rows + members : (n + 1) * rows, :] for n in range(4)]
        x = jnp.broadcast_to(r[1:2], (members, LANES))
        y = jnp.broadcast_to(r[2:3], (members, LANES))
        for _ in range(2):
            mx = x + 0.5 * STEP * bilinear(cx, x, y)
            my = y + 0.5 * STEP * bilinear(cy, x, y)
            x = x + STEP * bilinear(cx, mx, my)
            y = y + STEP * bilinear(cy, mx, my)
        lanes = pl.ds(pl.multiple_of(b * LANES, LANES), LANES)
        pred_ref[s, 0:members, lanes] = x
        pred_ref[s, members:rows, lanes] = y
        valid = r[6:7] > 0.5
        deviation = jnp.where(valid, r[5:6], 1.0)
        scale = jnp.where(valid, 1.0 / (deviation * spread), 0.0)
        inverse = jnp.where(valid, 1.0 / deviation, 0.0)
        mean_x = jnp.sum(x, axis=0, keepdims=True) * (1.0 / members)
        mean_y = jnp.sum(y, axis=0, keepdims=True) * (1.0 / members)
        anomaly = jnp.concatenate([(x - mean_x) * scale, (y - mean_y) * scale], axis=1)
        innovation = jnp.concatenate([(r[3:4] - mean_x) * inverse, (r[4:5] - mean_y) * inverse], axis=1)
        first = iota((8, 2 * LANES), 0) == 0
        both = jnp.concatenate([anomaly, jnp.where(first, innovation, 0.0)], axis=0)
        gram_ref[:, 0 : members + 8] += lax.dot_general(anomaly, both, NT, precision=HIGHEST, preferred_element_type=F32)

    def one_source(s, carry):
        amount = block_count(req_ref[s, 7:8, :])
        lax.fori_loop(0, amount, lambda b, c: (one_block(s, b), c)[1], 0)
        return carry

    lax.fori_loop(0, sources, one_source, 0)


def observe(zero, requests, members, local):
    sources, per, _ = requests.shape
    rows, width = zero.shape
    return pl.pallas_call(
        functools.partial(observe_kernel, members, local),
        in_specs=[vmem()] * 2,
        out_specs=[vmem()] * 2,
        out_shape=[
            jax.ShapeDtypeStruct((sources, rows, per // 8 * LANES), F32),
            jax.ShapeDtypeStruct((members, LANES), F32),
        ],
        scratch_shapes=[pltpu.VMEM((4 * rows, width), BF16), pltpu.VMEM((4 * rows, LANES), F32)],
        name="observe",
    )(zero, requests)


def all_sum(x):
    for axis in ("tile", "mem"):
        size = lax.axis_size(axis)
        bit = 1
        while bit < size:
            if size // bit >= 4 and not (axis == "tile" and bit == 1):
                a, b, c = [lax.ppermute(x, axis, [(n, n ^ (bit * k)) for n in range(size)]) for k in (1, 2, 3)]
                x = (x + a) + (b + c)
                bit *= 4
            else:
                x = x + lax.ppermute(x, axis, [(n, n ^ bit) for n in range(size)])
                bit *= 2
    return x


def ensemble_weights(gram_matrix, projection):
    members = gram_matrix.shape[0]
    identity = jnp.eye(members, dtype=F32)
    factor = jnp.linalg.cholesky(identity + gram_matrix)
    half_solve = lax.linalg.triangular_solve(factor, projection[:, None], left_side=True, lower=True)
    mean_weight = lax.linalg.triangular_solve(factor, half_solve, left_side=True, lower=True, transpose_a=True)
    inverse_root = lax.linalg.triangular_solve(factor, identity, left_side=True, lower=True, transpose_a=True)
    combined = mean_weight + jnp.sqrt(F32(members - 1)) * inverse_root
    return combined - jnp.mean(combined, axis=0, keepdims=True) + 1.0 / members


def spread_kernel(members, local, levels, w_ref, rest_ref, zero0_ref, zero1_ref, pos_ref):
    other = levels - 1
    weights = w_ref[...]
    rows = members * levels
    i = iota((rows, members), 0)
    repeat = ones_where(quotient(i, levels) == iota((rows, members), 1))
    tall = lax.dot_general(repeat, weights.astype(BF16), NT, preferred_element_type=F32).astype(BF16)
    cols = members * other
    j = iota((members, cols), 1)
    k = iota((members, cols), 0)
    widen = ones_where(jnp.logical_and(j >= k * other, j < (k + 1) * other))
    wide = jnp.dot(tall, widen, preferred_element_type=F32)
    i = iota((rows, cols), 0)
    j = iota((rows, cols), 1)
    same = i - quotient(i, levels) * levels == j - quotient(j, other) * other + 1
    rest_ref[...] = jnp.where(same, wide, 0.0).astype(BF16)
    j = iota((members, 2 * members), 1)
    k = iota((members, 2 * members), 0)
    source = quotient(k, local)
    i = iota((rows, 2 * members), 0)
    level0 = i - quotient(i, levels) * levels == 0
    for c, ref in enumerate((zero0_ref, zero1_ref)):
        move = ones_where(j == source * 2 * local + c * local + k - source * local)
        ref[...] = jnp.where(level0, jnp.dot(tall, move, preferred_element_type=F32), 0.0).astype(BF16)
    i = iota((2 * members, members), 0)
    half = quotient(i, 2)
    repeat = ones_where(half == iota((2 * members, members), 1), F32)
    tall = lax.dot_general(repeat, weights, NT, precision=HIGHEST, preferred_element_type=F32)
    odd = i - 2 * half == 1
    pos_ref[:, :members] = jnp.where(odd, 0.0, tall)
    pos_ref[:, members:] = jnp.where(odd, tall, 0.0)


def spread_weights(weights, local, levels):
    members = weights.shape[0]
    rows = members * levels
    return pl.pallas_call(
        functools.partial(spread_kernel, members, local, levels),
        in_specs=[vmem()],
        out_specs=[vmem()] * 4,
        out_shape=[
            jax.ShapeDtypeStruct((rows, members * (levels - 1)), BF16),
            jax.ShapeDtypeStruct((rows, 2 * members), BF16),
            jax.ShapeDtypeStruct((rows, 2 * members), BF16),
            jax.ShapeDtypeStruct((2 * members, 2 * members), F32),
        ],
        name="spread",
    )(weights)


def mix_kernel(share, rest_ref, zero_ref, w_rest_ref, w_zero_ref, out_ref):
    total = jnp.dot(w_rest_ref[...], rest_ref[...], preferred_element_type=F32)
    total += jnp.dot(w_zero_ref[...], zero_ref[:, :share], preferred_element_type=F32)
    out_ref[...] = total.astype(BF16)


def mix(rest, zero, w_rest, w_zero):
    share = rest.shape[1]
    return pl.pallas_call(
        functools.partial(mix_kernel, share),
        in_specs=[vmem()] * 4,
        out_specs=vmem(),
        out_shape=jax.ShapeDtypeStruct((w_rest.shape[0], share), BF16),
        name="mix",
    )(rest, zero, w_rest, w_zero)


def join_kernel(in0_ref, in1_ref, out_ref):
    out_ref[:, 0] = in0_ref[0]
    out_ref[:, 1] = in1_ref[0]


def join(part0, part1):
    shares, local, levels, share = part0.shape
    spec = pl.BlockSpec((1, local, levels, share), lambda q: (q, 0, 0, 0))
    return pl.pallas_call(
        join_kernel,
        grid=(shares,),
        in_specs=[spec, spec],
        out_specs=pl.BlockSpec((local, 2, levels, share), lambda q: (0, 0, 0, q)),
        out_shape=jax.ShapeDtypeStruct((local, 2, levels, shares * share), BF16),
        name="join",
    )(part0, part1)


def move_kernel(pred_ref, req_ref, w_ref, out_ref):
    sources, rows, _ = pred_ref.shape
    out_ref[...] = jnp.zeros_like(out_ref)

    def one_source(s, carry):
        amount = block_count(req_ref[s, 7:8, :])

        def one_block(b, c):
            lanes = pl.ds(pl.multiple_of(b * LANES, LANES), LANES)
            moved = jnp.dot(w_ref[...], pred_ref[s, :, lanes], precision=HIGHEST, preferred_element_type=F32)
            out_ref[s, :, lanes] = moved.astype(BF16)
            return c

        lax.fori_loop(0, amount, one_block, 0)
        return carry

    lax.fori_loop(0, sources, one_source, 0)


def move(pred, requests, w_pos):
    return pl.pallas_call(
        move_kernel,
        in_specs=[vmem()] * 3,
        out_specs=vmem(),
        out_shape=jax.ShapeDtypeStruct(pred.shape, BF16),
        name="move",
    )(pred, requests, w_pos)


def settle_kernel(back_ref, where_ref, count_ref, out_ref, acc_ref):
    tiles, rows, capacity = back_ref.shape
    drifters = where_ref.shape[1]
    acc_ref[...] = jnp.zeros_like(acc_ref)
    where_to = where_ref[...]

    def one_tile(t, carry):
        amount = block_count(count_ref[pl.ds(t, 1), :])

        def one_block(b, c):
            lanes = pl.ds(pl.multiple_of(b * LANES, LANES), LANES)
            slot = iota((LANES, drifters), 0) + (t * capacity + b * LANES)
            hit = ones_where(slot == where_to)
            acc_ref[...] += jnp.dot(back_ref[t, :, lanes], hit, preferred_element_type=F32)
            return c

        lax.fori_loop(0, amount, one_block, 0)
        return carry

    lax.fori_loop(0, tiles, one_tile, 0)
    out_ref[...] = acc_ref[...].astype(BF16)


def settle(back, where_to, count):
    _, rows, _ = back.shape
    drifters = where_to.shape[1]
    return pl.pallas_call(
        settle_kernel,
        in_specs=[vmem()] * 3,
        out_specs=vmem(),
        out_shape=jax.ShapeDtypeStruct((rows, drifters), BF16),
        scratch_shapes=[pltpu.VMEM((rows, drifters), F32)],
        name="settle",
    )(back, where_to, count)


def exchange(x, axis):
    return lax.all_to_all(x, axis, split_axis=0, concat_axis=0, tiled=True)


def shards(velocity, start_frac, observed, obs_sd, tile_of, cell_of):
    local, _, levels, cells = velocity.shape
    drifters = cell_of.shape[0]
    tiles = lax.axis_size("tile")
    shares = lax.axis_size("mem")
    members = local * shares
    share = cells // shares
    blocks = pl.cdiv(2 * drifters // tiles, LANES)

    zero, rest0, rest1 = pack(velocity, shares)
    zero = exchange(zero, "mem").reshape(2 * members, share + LANES)
    requests, where_to, count = route(
        lax.axis_index("mem"), tile_of, cell_of, start_frac, observed, obs_sd, tiles, blocks, share
    )
    requests = exchange(requests, "tile")
    rest0 = exchange(rest0, "mem").reshape(members * (levels - 1), share)
    rest1 = exchange(rest1, "mem").reshape(members * (levels - 1), share)
    pred, gram = observe(zero, requests, members, local)
    gram = all_sum(gram)
    weights = ensemble_weights(gram[:, :members], gram[:, members])
    w_rest, w_zero0, w_zero1, w_pos = spread_weights(weights, local, levels)

    mixed0 = mix(rest0, zero, w_rest, w_zero0).reshape(shares, local, levels, share)
    mixed0 = exchange(mixed0, "mem")
    moved = exchange(move(pred, requests, w_pos), "tile")
    mixed1 = mix(rest1, zero, w_rest, w_zero1).reshape(shares, local, levels, share)
    mixed1 = exchange(mixed1, "mem")
    settled = settle(moved, where_to, count).reshape(shares, 2 * local, drifters)
    settled = exchange(settled, "mem")
    new_positions = jnp.sum(settled.astype(F32), axis=0).reshape(local, 2, drifters)
    return join(mixed0, mixed1), new_positions


def solution(mesh):
    in_specs = (
        P("mem", None, None, "tile"),
        P(None, "tile"),
        P(None, "tile"),
        P("tile"),
        P("tile", None),
        P("tile"),
    )
    out_specs = (P("mem", None, None, "tile"), P("mem", None, "tile"))
    return jax.shard_map(shards, mesh=mesh, in_specs=in_specs, out_specs=out_specs, check_vma=False)
```

profile of v0, /device:TPU:0, one launch (start us, length us, event | category | flops | bytes accessed | tf_op | source)
XLA Modules:
  0.0 271.2 jit_solution(16294326790579538623)
XLA Ops:
  0.6 3.6 %route.1 = (f32[8,32,128]{2,1,0:T(8,128)}, s32[1,2048]{1,0:T(1,128)}, f32[8,128]{1,0:T(8,128)}) custom-call(s32[1]{0:T(128)} %bitcast.3.q_ref, s32[1,2048]{1,0:T(1,128)} %bitcast.45, s32[1,2048]{1,0:T(1,128)} %bitcast.46, f32[2,2048]{1,0:T(2,128)} %frac_ref.1, f32[2,2048]{1,0:T(2,128)} %obs_ref.1, f32[1,2048]{1,0:T(1,128)} %bitcast.47), custom_call_target="tpu_custom_call" | custom-call | tf_op jit(solution)/shard_map/route/pallas_call | solution.py:119
  4.2 5.2 %all-to-all-start.2 = ((f32[8,32,128]{2,1,0:T(8,128)}), f32[8,32,128]{2,1,0:T(8,128)S(1)}, u32[]{:S(2)}, u32[]{:S(2)}) async-start(f32[8,32,128]{2,1,0:T(8,128)} %get-tuple-element.16), calls=%async_computation.2 | async-start | bytes 262144 | tf_op jit(solution)/shard_map/all_to_all | solution.py:393
  9.4 5.4 %pack.1 = (bf16[4,48,1152]{2,1,0:T(8,128)(2,1)}, bf16[4,168,1024]{2,1,0:T(8,128)(2,1)}, bf16[4,168,1024]{2,1,0:T(8,128)(2,1)}) custom-call(bf16[384,4096]{1,0:T(8,128)(2,1)} %bitcast.35, bf16[384,4096]{1,0:T(8,128)(2,1)} %bitcast.36), custom_call_target="tpu_custom_call" | custom-call | tf_op jit(solution)/shard_map/pack/pallas_call | solution.py:64
  14.8 0.1 all-to-all-done.2.req_ref
  14.9 0.0 copy-start.5
  14.9 18.3 %all_to_all.40 = bf16[4,48,1152]{2,1,0:T(8,128)(2,1)} all-to-all(bf16[4,48,1152]{2,1,0:T(8,128)(2,1)} %get-tuple-element.15), channel_id=1, replica_groups=mesh['tile'=8,'mem'=4] {'mem'}, dimensions={0} | all-to-all | bytes 884736 | tf_op jit(solution)/shard_map/all_to_all | solution.py:393
  33.2 0.0 copy-done.5
  33.2 13.5 %observe.1 = (f32[8,192,512]{2,1,0:T(8,128)}, f32[96,128]{1,0:T(8,128)}) custom-call(bf16[192,1152]{1,0:T(8,128)(2,1)} %bitcast.37, f32[8,32,128]{2,1,0:T(8,128)} %copy-done.5), custom_call_target="tpu_custom_call" | custom-call | tf_op jit(solution)/shard_map/observe/pallas_call | solution.py:203
  46.7 0.0 collective-permute-start
  46.7 1.4 collective-permute-done
  48.1 0.8 add.53
  48.9 7.1 %collective-permute-start.3 = (f32[96,128]{1,0:T(8,128)S(1)}, f32[96,128]{1,0:T(8,128)S(1)}, u32[]{:S(2)}, u32[]{:S(2)}) collective-permute-start(f32[96,128]{1,0:T(8,128)S(1)} %add.53), channel_id=1, source_target_pairs={{0,24},{4,28},{8,16},{12,20},{16,8},{20,12},{24,0},{28,4},{1,25},{... | collective-permute-start | bytes 147464 | tf_op jit(solution)/shard_map/ppermute | solution.py:222
  56.0 0.0 collective-permute-start.2
  56.0 0.6 collective-permute-start.1
  56.7 1.6 collective-permute-done.3
  58.3 1.8 collective-permute-done.2
  60.1 0.0 collective-permute-done.1
  60.1 0.1 collective-permute-start.6
  60.2 1.6 collective-permute-start.5
  61.8 2.8 %collective-permute-start.4 = (f32[96,128]{1,0:T(8,128)S(1)}, f32[96,128]{1,0:T(8,128)S(1)}, u32[]{:S(2)}, u32[]{:S(2)}) collective-permute-start(f32[96,128]{1,0:T(8,128)S(1)} %add_add_fusion.1), channel_id=1, source_target_pairs={{0,1},{1,0},{2,3},{3,2},{4,5},{5,4},{6,7},{7,6},{8,9},{9,8},{10,11... | collective-permute-start | bytes 147464 | tf_op jit(solution)/shard_map/ppermute | solution.py:222
  64.6 3.5 %all-to-all-start = ((bf16[4,168,1024]{2,1,0:T(8,128)(2,1)}), bf16[4,168,1024]{2,1,0:T(8,128)(2,1)S(1)}, u32[]{:S(2)}, u32[]{:S(2)}) async-start(bf16[4,168,1024]{2,1,0:T(8,128)(2,1)} %get-tuple-element.14), calls=%async_computation | async-start | bytes 2752512 | tf_op jit(solution)/shard_map/all_to_all | solution.py:393
  68.1 0.0 collective-permute-done.6
  68.1 0.0 collective-permute-done.5
  68.2 0.0 collective-permute-done.4
  68.2 0.1 copy.9
  68.3 8.8 %cholesky.18 = f32[96,96]{1,0:T(8,128)S(1)} custom-call(f32[96,96]{1,0:T(8,128)S(1)} %fusion.5), custom_call_target="Cholesky" | custom-call | tf_op jit(solution)/shard_map/jit(cholesky)/cholesky | solution.py:234
  77.1 0.6 compare_reduce_fusion
  77.8 0.7 fusion.1
  78.4 7.4 %custom-call.10 = f32[1,96,96]{1,2,0:T(8,128)S(1)} custom-call(f32[1,96,96]{2,1,0:T(8,128)S(1)} %fusion.1), custom_call_target="InvertDiagBlocksLowerTriangular" | custom-call | tf_op jit(solution)/shard_map/triangular_solve | solution.py:236
  85.8 0.2 slice_reduce_fusion
  86.0 0.2 convolution_bitcast_fusion.1
  86.1 0.2 convolution_bitcast_fusion
  86.3 0.2 fusion.7
  86.5 0.6 subtract_add_fusion.w_ref
  87.2 2.9 %spread.1 = (bf16[768,672]{1,0:T(8,128)(2,1)}, bf16[768,192]{1,0:T(8,128)(2,1)}, bf16[768,192]{1,0:T(8,128)(2,1)}, f32[192,192]{1,0:T(8,128)}) custom-call(f32[96,96]{1,0:T(8,128)} %subtract_add_fusion.w_ref), custom_call_target="tpu_custom_call" | custom-call | tf_op jit(solution)/shard_map/spread/pallas_call | solution.py:278
  90.1 6.8 %move.1 = bf16[8,192,512]{2,1,0:T(8,128)(2,1)} custom-call(f32[8,192,512]{2,1,0:T(8,128)} %get-tuple-element.22.pred_ref, f32[8,32,128]{2,1,0:T(8,128)} %copy-done.5, f32[192,192]{1,0:T(8,128)} %get-tuple-element.23.w_ref), custom_call_target="tpu_custom_call" | custom-call | tf_op jit(solution)/shard_map/move/pallas_call | solution.py:347
  96.8 2.5 all-to-all-done
  99.4 0.0 copy-start.2
  99.4 25.2 %all_to_all.41.back_ref = bf16[8,192,512]{2,1,0:T(8,128)(2,1)} all-to-all(bf16[8,192,512]{2,1,0:T(8,128)(2,1)} %move.1), channel_id=1, replica_groups=mesh['tile'=8,'mem'=4] {'tile'}, dimensions={0} | all-to-all | bytes 3145728 | tf_op jit(solution)/shard_map/all_to_all | solution.py:393
  124.6 0.0 copy-done.2
  124.6 3.5 %all-to-all-start.4 = ((bf16[4,168,1024]{2,1,0:T(8,128)(2,1)}), bf16[4,168,1024]{2,1,0:T(8,128)(2,1)S(1)}, u32[]{:S(2)}, u32[]{:S(2)}) async-start(bf16[4,168,1024]{2,1,0:T(8,128)(2,1)} %get-tuple-element.20), calls=%async_computation.4 | async-start | bytes 2752512 | tf_op jit(solution)/shard_map/all_to_all | solution.py:393
  128.2 6.4 %settle.1 = bf16[192,2048]{1,0:T(8,128)(2,1)} custom-call(bf16[8,192,512]{2,1,0:T(8,128)(2,1)} %all_to_all.41.back_ref, s32[1,2048]{1,0:T(1,128)} %get-tuple-element.24.where_ref, f32[8,128]{1,0:T(8,128)} %get-tuple-element.25.count_ref), custom_call_target="tpu_custom_call" | custom-call | tf_op jit(solution)/shard_map/settle/pallas_call | solution.py:382
  134.5 26.0 %all-to-all-done.4 = bf16[4,168,1024]{2,1,0:T(8,128)(2,1)S(1)} async-done(((bf16[4,168,1024]{2,1,0:T(8,128)(2,1)}), bf16[4,168,1024]{2,1,0:T(8,128)(2,1)S(1)}, u32[]{:S(2)}, u32[]{:S(2)}) %all-to-all-start.4) | async-done | bytes 1376288 | tf_op jit(solution)/shard_map/all_to_all | solution.py:393
  160.6 0.0 copy-start.3
  160.6 3.7 %all-to-all-start.7 = ((bf16[4,48,2048]{2,1,0:T(8,128)(2,1)}), bf16[4,48,2048]{2,1,0:T(8,128)(2,1)S(1)}, u32[]{:S(2)}, u32[]{:S(2)}) async-start(bf16[4,48,2048]{2,1,0:T(8,128)(2,1)} %bitcast.44), calls=%async_computation.7 | async-start | bytes 1572864 | tf_op jit(solution)/shard_map/all_to_all | solution.py:393
  164.3 4.8 %mix.2 = bf16[768,1024]{1,0:T(8,128)(2,1)} custom-call(bf16[672,1024]{1,0:T(8,128)(2,1)} %bitcast.42, bf16[192,1152]{1,0:T(8,128)(2,1)} %bitcast.38, bf16[768,672]{1,0:T(8,128)(2,1)} %get-tuple-element.18.w_rest_ref, bf16[768,192]{1,0:T(8,128)(2,1)} %get-tuple-element.19.w_zero_ref), custom_call_target="tpu_custom_call" | custom-call | tf_op jit(solution)/shard_map/mix/pallas_call | solution.py:300
  169.1 0.0 copy-done.3
  169.1 14.6 %all-to-all-done.7 = bf16[4,48,2048]{2,1,0:T(8,128)(2,1)S(1)} async-done(((bf16[4,48,2048]{2,1,0:T(8,128)(2,1)}), bf16[4,48,2048]{2,1,0:T(8,128)(2,1)S(1)}, u32[]{:S(2)}, u32[]{:S(2)}) %all-to-all-start.7) | async-done | bytes 786464 | tf_op jit(solution)/shard_map/all_to_all | solution.py:393
  183.7 0.0 copy-start.4
  183.7 0.9 copy-done.4
  184.6 3.6 %all-to-all-start.3 = ((bf16[4,24,8,1024]{3,2,1,0:T(8,128)(2,1)}), bf16[4,24,8,1024]{3,2,1,0:T(8,128)(2,1)S(1)}, u32[]{:S(2)}, u32[]{:S(2)}) async-start(bf16[4,24,8,1024]{3,2,1,0:T(8,128)(2,1)} %bitcast.40), calls=%async_computation.3 | async-start | bytes 3145728 | tf_op jit(solution)/shard_map/all_to_all | solution.py:393
  188.2 4.8 %mix.3 = bf16[768,1024]{1,0:T(8,128)(2,1)} custom-call(bf16[672,1024]{1,0:T(8,128)(2,1)} %bitcast.43, bf16[192,1152]{1,0:T(8,128)(2,1)} %bitcast.39, bf16[768,672]{1,0:T(8,128)(2,1)} %get-tuple-element.18.w_rest_ref, bf16[768,192]{1,0:T(8,128)(2,1)} %get-tuple-element.21.w_zero_ref), custom_call_target="tpu_custom_call" | custom-call | tf_op jit(solution)/shard_map/mix/pallas_call | solution.py:300
  193.1 31.6 %all-to-all-done.3.in0_ref = bf16[4,24,8,1024]{3,2,1,0:T(8,128)(2,1)S(1)} async-done(((bf16[4,24,8,1024]{3,2,1,0:T(8,128)(2,1)}), bf16[4,24,8,1024]{3,2,1,0:T(8,128)(2,1)S(1)}, u32[]{:S(2)}, u32[]{:S(2)}) %all-to-all-start.3) | async-done | bytes 1572896 | tf_op jit(solution)/shard_map/all_to_all | solution.py:393
  224.7 0.0 copy-start
  224.7 1.1 copy-done
  225.8 3.6 %all-to-all-start.5 = ((bf16[4,24,8,1024]{3,2,1,0:T(8,128)(2,1)}), bf16[4,24,8,1024]{3,2,1,0:T(8,128)(2,1)S(1)}, u32[]{:S(2)}, u32[]{:S(2)}) async-start(bf16[4,24,8,1024]{3,2,1,0:T(8,128)(2,1)} %bitcast.41), calls=%async_computation.5 | async-start | bytes 3145728 | tf_op jit(solution)/shard_map/all_to_all | solution.py:393
  229.4 1.3 convert_reduce_fusion
  230.7 1.0 reshape.77
  231.7 34.2 %all-to-all-done.5.in1_ref = bf16[4,24,8,1024]{3,2,1,0:T(8,128)(2,1)S(1)} async-done(((bf16[4,24,8,1024]{3,2,1,0:T(8,128)(2,1)}), bf16[4,24,8,1024]{3,2,1,0:T(8,128)(2,1)S(1)}, u32[]{:S(2)}, u32[]{:S(2)}) %all-to-all-start.5) | async-done | bytes 1572896 | tf_op jit(solution)/shard_map/all_to_all | solution.py:393
  265.9 0.0 copy-start.1
  265.9 1.2 copy-done.1
  267.0 4.1 %join.1 = bf16[24,2,8,4096]{3,2,1,0:T(8,128)(2,1)} custom-call(bf16[4,24,8,1024]{3,2,1,0:T(8,128)(2,1)} %copy-done, bf16[4,24,8,1024]{3,2,1,0:T(8,128)(2,1)} %copy-done.1), custom_call_target="tpu_custom_call" | custom-call | tf_op jit(solution)/shard_map/join/pallas_call | solution.py:317
  (6 shorter events, 0.1 us)
Async XLA Ops:
  4.2 10.7 %all-to-all-start.2 = ((f32[8,32,128]{2,1,0:T(8,128)}), f32[8,32,128]{2,1,0:T(8,128)S(1)}, u32[]{:S(2)}, u32[]{:S(2)}) async-start(f32[8,32,128]{2,1,0:T(8,128)} %get-tuple-element.16), calls=%async_computation.2 | async-start | bytes 262144 | tf_op jit(solution)/shard_map/all_to_all | solution.py:393
  14.9 18.3 %copy-start.5 = (f32[8,32,128]{2,1,0:T(8,128)}, f32[8,32,128]{2,1,0:T(8,128)S(1)}, u32[]{:S(2)}) copy-start(f32[8,32,128]{2,1,0:T(8,128)S(1)} %all-to-all-done.2.req_ref) | copy-start | bytes 393220
  46.7 1.4 collective-permute-start
  48.9 9.3 %collective-permute-start.3 = (f32[96,128]{1,0:T(8,128)S(1)}, f32[96,128]{1,0:T(8,128)S(1)}, u32[]{:S(2)}, u32[]{:S(2)}) collective-permute-start(f32[96,128]{1,0:T(8,128)S(1)} %add.53), channel_id=1, source_target_pairs={{0,24},{4,28},{8,16},{12,20},{16,8},{20,12},{24,0},{28,4},{1,25},{... | collective-permute-start | bytes 147464 | tf_op jit(solution)/shard_map/ppermute | solution.py:222
  56.0 4.1 %collective-permute-start.2 = (f32[96,128]{1,0:T(8,128)S(1)}, f32[96,128]{1,0:T(8,128)S(1)}, u32[]{:S(2)}, u32[]{:S(2)}) collective-permute-start(f32[96,128]{1,0:T(8,128)S(1)} %add.53), channel_id=1, source_target_pairs={{0,16},{4,20},{8,24},{12,28},{16,0},{20,4},{24,8},{28,12},{1,17},{... | collective-permute-start | bytes 147464 | tf_op jit(solution)/shard_map/ppermute | solution.py:222
  56.0 4.1 %collective-permute-start.1 = (f32[96,128]{1,0:T(8,128)S(1)}, f32[96,128]{1,0:T(8,128)S(1)}, u32[]{:S(2)}, u32[]{:S(2)}) collective-permute-start(f32[96,128]{1,0:T(8,128)S(1)} %add.53), channel_id=1, source_target_pairs={{0,8},{4,12},{8,0},{12,4},{16,24},{20,28},{24,16},{28,20},{1,9},{5... | collective-permute-start | bytes 147464 | tf_op jit(solution)/shard_map/ppermute | solution.py:222
  60.1 8.0 %collective-permute-start.6 = (f32[96,128]{1,0:T(8,128)S(1)}, f32[96,128]{1,0:T(8,128)S(1)}, u32[]{:S(2)}, u32[]{:S(2)}) collective-permute-start(f32[96,128]{1,0:T(8,128)S(1)} %add_add_fusion.1), channel_id=1, source_target_pairs={{0,3},{1,2},{2,1},{3,0},{4,7},{5,6},{6,5},{7,4},{8,11},{9,10},{10,... | collective-permute-start | bytes 147464 | tf_op jit(solution)/shard_map/ppermute | solution.py:222
  60.2 7.9 %collective-permute-start.5 = (f32[96,128]{1,0:T(8,128)S(1)}, f32[96,128]{1,0:T(8,128)S(1)}, u32[]{:S(2)}, u32[]{:S(2)}) collective-permute-start(f32[96,128]{1,0:T(8,128)S(1)} %add_add_fusion.1), channel_id=1, source_target_pairs={{0,2},{1,3},{2,0},{3,1},{4,6},{5,7},{6,4},{7,5},{8,10},{9,11},{10,... | collective-permute-start | bytes 147464 | tf_op jit(solution)/shard_map/ppermute | solution.py:222
  61.8 6.4 %collective-permute-start.4 = (f32[96,128]{1,0:T(8,128)S(1)}, f32[96,128]{1,0:T(8,128)S(1)}, u32[]{:S(2)}, u32[]{:S(2)}) collective-permute-start(f32[96,128]{1,0:T(8,128)S(1)} %add_add_fusion.1), channel_id=1, source_target_pairs={{0,1},{1,0},{2,3},{3,2},{4,5},{5,4},{6,7},{7,6},{8,9},{9,8},{10,11... | collective-permute-start | bytes 147464 | tf_op jit(solution)/shard_map/ppermute | solution.py:222
  64.6 34.8 %all-to-all-start = ((bf16[4,168,1024]{2,1,0:T(8,128)(2,1)}), bf16[4,168,1024]{2,1,0:T(8,128)(2,1)S(1)}, u32[]{:S(2)}, u32[]{:S(2)}) async-start(bf16[4,168,1024]{2,1,0:T(8,128)(2,1)} %get-tuple-element.14), calls=%async_computation | async-start | bytes 2752512 | tf_op jit(solution)/shard_map/all_to_all | solution.py:393
  99.4 25.2 %copy-start.2 = (bf16[4,168,1024]{2,1,0:T(8,128)(2,1)}, bf16[4,168,1024]{2,1,0:T(8,128)(2,1)S(1)}, u32[]{:S(2)}) copy-start(bf16[4,168,1024]{2,1,0:T(8,128)(2,1)S(1)} %all-to-all-done) | copy-start | bytes 4128772
  124.6 36.0 %all-to-all-start.4 = ((bf16[4,168,1024]{2,1,0:T(8,128)(2,1)}), bf16[4,168,1024]{2,1,0:T(8,128)(2,1)S(1)}, u32[]{:S(2)}, u32[]{:S(2)}) async-start(bf16[4,168,1024]{2,1,0:T(8,128)(2,1)} %get-tuple-element.20), calls=%async_computation.4 | async-start | bytes 2752512 | tf_op jit(solution)/shard_map/all_to_all | solution.py:393
  160.6 8.5 %copy-start.3 = (bf16[4,168,1024]{2,1,0:T(8,128)(2,1)}, bf16[4,168,1024]{2,1,0:T(8,128)(2,1)S(1)}, u32[]{:S(2)}) copy-start(bf16[4,168,1024]{2,1,0:T(8,128)(2,1)S(1)} %all-to-all-done.4) | copy-start | bytes 4128772
  160.6 23.1 %all-to-all-start.7 = ((bf16[4,48,2048]{2,1,0:T(8,128)(2,1)}), bf16[4,48,2048]{2,1,0:T(8,128)(2,1)S(1)}, u32[]{:S(2)}, u32[]{:S(2)}) async-start(bf16[4,48,2048]{2,1,0:T(8,128)(2,1)} %bitcast.44), calls=%async_computation.7 | async-start | bytes 1572864 | tf_op jit(solution)/shard_map/all_to_all | solution.py:393
  183.7 0.9 copy-start.4
  184.6 40.1 %all-to-all-start.3 = ((bf16[4,24,8,1024]{3,2,1,0:T(8,128)(2,1)}), bf16[4,24,8,1024]{3,2,1,0:T(8,128)(2,1)S(1)}, u32[]{:S(2)}, u32[]{:S(2)}) async-start(bf16[4,24,8,1024]{3,2,1,0:T(8,128)(2,1)} %bitcast.40), calls=%async_computation.3 | async-start | bytes 3145728 | tf_op jit(solution)/shard_map/all_to_all | solution.py:393
  224.7 1.1 copy-start
  225.8 40.1 %all-to-all-start.5 = ((bf16[4,24,8,1024]{3,2,1,0:T(8,128)(2,1)}), bf16[4,24,8,1024]{3,2,1,0:T(8,128)(2,1)S(1)}, u32[]{:S(2)}, u32[]{:S(2)}) async-start(bf16[4,24,8,1024]{3,2,1,0:T(8,128)(2,1)} %bitcast.41), calls=%async_computation.5 | async-start | bytes 3145728 | tf_op jit(solution)/shard_map/all_to_all | solution.py:393
  265.9 1.2 copy-start.1
where the time goes:
time: 272 us; the launch traced here: 271 us
  waiting for transfers between devices  114 us (42%)
  Pallas kernels  52.3 us (19%)
  blocking collectives  43.5 us (16%)
  starting transfers between devices  35.3 us (13%)
  other arithmetic  20.3 us (7%)
  local copies, waits for them, and re-layouts  4.44 us (2%)
    all_to_all x6, waiting for transfers between devices, exchange(): return lax.all_to_all(x, axis, split_axis=0, concat_axis=0, tiled=True)  109 us
    all_to_all x2, blocking collectives, exchange(): return lax.all_to_all(x, axis, split_axis=0, concat_axis=0, tiled=True)  43.5 us
    all_to_all x6, starting transfers between devices, exchange(): return lax.all_to_all(x, axis, split_axis=0, concat_axis=0, tiled=True)  23.1 us
    pallas_call x1, Pallas kernels, observe(): pl.pallas_call(functools.partial(observe_kernel, members, local), in_spec...  13.5 us
    ppermute x6, starting transfers between devices, all_sum(): lax.ppermute(x, axis, [(n, n ^ bit * k) for n in range(size)])  12.2 us
    pallas_call x2, Pallas kernels, mix(): pl.pallas_call(functools.partial(mix_kernel, share), in_specs=[vmem()] *...  9.67 us
    another operation x3, other arithmetic, ensemble_weights(): factor = jnp.linalg.cholesky(identity + gram_matrix)  9.45 us
    another operation x2, other arithmetic, ensemble_weights(): lax.linalg.triangular_solve(factor, half_solve, left_side=True, lower=Tru...  8.01 us
  transfers between devices with their start and end apart: 13, of which 9 were waited for; matrix products, arithmetic and copies ran while one was open for 8% of the time, Pallas kernels for 11%

commit v1 on v0

v1 whole, which is shorter than its diff:
```python
import functools
import math

import jax
import jax.numpy as jnp
from jax import lax
from jax.experimental import pallas as pl
from jax.experimental.pallas import tpu as pltpu
from jax.sharding import PartitionSpec as P


BX = 64
LANES = 128
STEP = 0.2
BF16 = jnp.bfloat16
F32 = jnp.float32
I32 = jnp.int32
HIGHEST = lax.Precision.HIGHEST
NT = (((1,), (1,)), ((), ()))


def iota(shape, dim):
    return lax.broadcasted_iota(I32, shape, dim)


def quotient(values, divisor):
    return ((values.astype(F32) + 0.5) * (1.0 / divisor)).astype(I32)


def ones_where(mask, dtype=BF16):
    return jnp.where(mask, 1.0, 0.0).astype(dtype)


def vmem():
    return pl.BlockSpec(memory_space=pltpu.VMEM)


def smem():
    return pl.BlockSpec(memory_space=pltpu.SMEM)


def round_up(value, unit):
    return pl.cdiv(value, unit) * unit


def pack_zero_kernel(local, levels, share, z_ref, v_ref, *out_refs):
    rows, cells = v_ref.shape
    i = iota((2 * local, rows), 0)
    j = iota((2 * local, rows), 1)
    comp = (i >= local).astype(I32)
    pick = ones_where(j == ((i - comp * local) * 2 + comp) * levels)
    for r, ref in enumerate(out_refs):
        start = (z_ref[0] ^ r) * share
        after = jnp.minimum(start + share, cells - LANES)
        x = v_ref[:, pl.ds(pl.multiple_of(start, LANES), share)]
        ref[:, :share] = jnp.dot(pick, x, preferred_element_type=F32).astype(BF16)
        x = v_ref[:, pl.ds(pl.multiple_of(after, LANES), LANES)]
        ref[:, share:] = jnp.dot(pick, x, preferred_element_type=F32).astype(BF16)


def pack_rest_kernel(local, levels, share, comp, z_ref, v_ref, *out_refs):
    rows, _ = v_ref.shape
    other = levels - 1
    i = iota((other * local, rows), 0)
    j = iota((other * local, rows), 1)
    member = quotient(i, other)
    pick = ones_where(j == (member * 2 + comp) * levels + (i - member * other) + 1)
    for r, ref in enumerate(out_refs):
        start = (z_ref[0] ^ r) * share
        x = v_ref[:, pl.ds(pl.multiple_of(start, LANES), share)]
        ref[...] = jnp.dot(pick, x, preferred_element_type=F32).astype(BF16)


def pack(z, velocity, shares):
    local, _, levels, cells = velocity.shape
    share = cells // shares
    flat = velocity.reshape(local * 2 * levels, cells)
    other = (levels - 1) * local

    def call(kernel, shape):
        return pl.pallas_call(
            kernel,
            in_specs=[smem(), vmem()],
            out_specs=[vmem()] * shares,
            out_shape=[jax.ShapeDtypeStruct(shape, BF16)] * shares,
        )(z, flat)

    zero = call(functools.partial(pack_zero_kernel, local, levels, share), (2 * local, share + LANES))
    rest = [call(functools.partial(pack_rest_kernel, local, levels, share, c), (other, share)) for c in range(2)]
    return zero, rest


def route_kernel(tiles, blocks, share, q_ref, tile_ref, cell_ref, frac_ref, obs_ref, sd_ref, req_ref, where_ref, count_ref):
    drifters = cell_ref.shape[1]
    dest = tile_ref[...]
    local_cell = cell_ref[...] - q_ref[0] * share
    mine = jnp.logical_and(local_cell >= 0, local_cell < share)
    named = jnp.where(jnp.logical_and(iota((tiles, drifters), 0) == dest, mine), 1.0, 0.0)
    upper = ones_where(iota((LANES, LANES), 0) <= iota((LANES, LANES), 1))
    before = jnp.zeros((tiles, 1), F32)
    sums = []
    for start in range(0, drifters, LANES):
        part = named[:, start : start + LANES]
        sums.append(jnp.dot(part.astype(BF16), upper, preferred_element_type=F32) + before)
        before = before + jnp.sum(part, axis=1, keepdims=True)
    running = jnp.concatenate(sums, axis=1)
    slot = jnp.sum(named * (running - 1.0), axis=0, keepdims=True).astype(I32)
    total = jnp.sum(named * before, axis=0, keepdims=True)
    where_to = jnp.where(mine, dest * (blocks * LANES) + slot, -1)
    where_ref[...] = where_to
    count_ref[...] = jnp.broadcast_to(before, count_ref.shape)
    payload = jnp.concatenate(
        [local_cell.astype(F32), frac_ref[...], obs_ref[...], sd_ref[...], jnp.ones_like(total), total], axis=0
    )
    high = lax.shift_right_arithmetic(where_to, int(math.log2(LANES)))
    low = jnp.bitwise_and(where_to, LANES - 1)
    spread = jnp.concatenate([jnp.where(high == h, payload, 0.0) for h in range(tiles * blocks)], axis=0)
    place = ones_where(iota((LANES, drifters), 0) == low, F32)
    placed = lax.dot_general(spread, place, NT, precision=HIGHEST, preferred_element_type=F32)
    per = 8 * blocks
    for t in range(tiles):
        req_ref[t] = placed[t * per : (t + 1) * per]


def route(q, tile_of, cell_of, start_frac, observed, obs_sd, tiles, blocks, share):
    drifters = cell_of.shape[0]
    return pl.pallas_call(
        functools.partial(route_kernel, tiles, blocks, share),
        in_specs=[smem()] + [vmem()] * 5,
        out_specs=[vmem()] * 3,
        out_shape=[
            jax.ShapeDtypeStruct((tiles, 8 * blocks, LANES), F32),
            jax.ShapeDtypeStruct((1, drifters), I32),
            jax.ShapeDtypeStruct((tiles, LANES), F32),
        ],
        name="route",
    )(
        q,
        tile_of.reshape(1, drifters),
        cell_of.reshape(1, drifters),
        start_frac,
        observed,
        obs_sd.reshape(1, drifters),
    )


def bilinear(corner, x, y):
    return (1.0 - x) * (1.0 - y) * corner[0] + x * (1.0 - y) * corner[1] + (1.0 - x) * y * corner[2] + x * y * corner[3]


def block_count(value):
    return lax.shift_right_arithmetic(jnp.max(value).astype(I32) + (LANES - 1), int(math.log2(LANES)))


def observe_kernel(members, local, z_ref, req_ref, *refs):
    zero_refs, (pred_ref, gram_ref, table_ref, corner_ref) = refs[:-4], refs[-4:]
    sources = req_ref.shape[0]
    rows, width = 2 * members, zero_refs[0].shape[1]
    i = iota((rows, 2 * local), 0)
    j = iota((rows, 2 * local), 1)
    comp = (j >= local).astype(I32)
    target = comp * members + j - comp * local
    table = jnp.zeros((rows, width), F32)
    for r, ref in enumerate(zero_refs):
        pick = ones_where(i == target + (z_ref[0] ^ r) * local)
        table += jnp.dot(pick, ref[...], preferred_element_type=F32)
    for n, offset in enumerate((0, 1, BX, BX + 1)):
        moved = table if offset == 0 else pltpu.roll(table, width - offset, 1)
        table_ref[n * rows : (n + 1) * rows, :] = moved.astype(BF16)
    gram_ref[...] = jnp.zeros_like(gram_ref)
    spread = math.sqrt(members - 1)

    def one_block(s, b):
        r = req_ref[s, pl.ds(pl.multiple_of(b * 8, 8), 8), :]
        cell = r[0:1].astype(I32)
        hit = ones_where(iota((width, LANES), 0) == cell)
        corner_ref[...] = jnp.dot(table_ref[...], hit, preferred_element_type=F32)
        cx = [corner_ref[n * rows : n * rows + members, :] for n in range(4)]
        cy = [corner_ref[n * rows + members : (n + 1) * rows, :] for n in range(4)]
        x = jnp.broadcast_to(r[1:2], (members, LANES))
        y = jnp.broadcast_to(r[2:3], (members, LANES))
        for _ in range(2):
            mx = x + 0.5 * STEP * bilinear(cx, x, y)
            my = y + 0.5 * STEP * bilinear(cy, x, y)
            x = x + STEP * bilinear(cx, mx, my)
            y = y + STEP * bilinear(cy, mx, my)
        lanes = pl.ds(pl.multiple_of(b * LANES, LANES), LANES)
        pred_ref[s, 0:members, lanes] = x
        pred_ref[s, members:rows, lanes] = y
        valid = r[6:7] > 0.5
        deviation = jnp.where(valid, r[5:6], 1.0)
        scale = jnp.where(valid, 1.0 / (deviation * spread), 0.0)
        inverse = jnp.where(valid, 1.0 / deviation, 0.0)
        mean_x = jnp.sum(x, axis=0, keepdims=True) * (1.0 / members)
        mean_y = jnp.sum(y, axis=0, keepdims=True) * (1.0 / members)
        anomaly = jnp.concatenate([(x - mean_x) * scale, (y - mean_y) * scale], axis=1)
        innovation = jnp.concatenate([(r[3:4] - mean_x) * inverse, (r[4:5] - mean_y) * inverse], axis=1)
        first = iota((8, 2 * LANES), 0) == 0
        both = jnp.concatenate([anomaly, jnp.where(first, innovation, 0.0)], axis=0)
        gram_ref[:, 0 : members + 8] += lax.dot_general(anomaly, both, NT, precision=HIGHEST, preferred_element_type=F32)

    def one_source(s, carry):
        amount = block_count(req_ref[s, 7:8, :])
        lax.fori_loop(0, amount, lambda b, c: (one_block(s, b), c)[1], 0)
        return carry

    lax.fori_loop(0, sources, one_source, 0)


def observe(z, zero, requests, members, local):
    sources, per, _ = requests.shape
    rows, width = 2 * members, zero[0].shape[1]
    return pl.pallas_call(
        functools.partial(observe_kernel, members, local),
        in_specs=[smem()] + [vmem()] * (1 + len(zero)),
        out_specs=[vmem()] * 2,
        out_shape=[
            jax.ShapeDtypeStruct((sources, rows, per // 8 * LANES), F32),
            jax.ShapeDtypeStruct((members, LANES), F32),
        ],
        scratch_shapes=[pltpu.VMEM((4 * rows, width), BF16), pltpu.VMEM((4 * rows, LANES), F32)],
        name="observe",
    )(z, requests, *zero)


def all_sum(x):
    for axis in ("tile", "mem"):
        size = lax.axis_size(axis)
        bit = 1
        while bit < size:
            if size // bit >= 4 and not (axis == "tile" and bit == 1):
                a, b, c = [lax.ppermute(x, axis, [(n, n ^ (bit * k)) for n in range(size)]) for k in (1, 2, 3)]
                x = (x + a) + (b + c)
                bit *= 4
            else:
                x = x + lax.ppermute(x, axis, [(n, n ^ bit) for n in range(size)])
                bit *= 2
    return x


def ensemble_weights(gram_matrix, projection):
    members = gram_matrix.shape[0]
    identity = jnp.eye(members, dtype=F32)
    factor = jnp.linalg.cholesky(identity + gram_matrix)
    half_solve = lax.linalg.triangular_solve(factor, projection[:, None], left_side=True, lower=True)
    mean_weight = lax.linalg.triangular_solve(factor, half_solve, left_side=True, lower=True, transpose_a=True)
    inverse_root = lax.linalg.triangular_solve(factor, identity, left_side=True, lower=True, transpose_a=True)
    combined = mean_weight + jnp.sqrt(F32(members - 1)) * inverse_root
    return combined - jnp.mean(combined, axis=0, keepdims=True) + 1.0 / members


def spread_kernel(members, local, levels, gap, z_ref, w_ref, mix0_ref, mix1_ref, pos_ref):
    z = z_ref[0]
    other = levels - 1
    weights = w_ref[...]

    def member_of(index, each):
        r = quotient(index, local * each)
        inside = quotient(index - r * local * each, each)
        return (r ^ z) * local + inside

    rows = members * levels
    i = iota((rows, members), 0)
    repeat = ones_where(member_of(i, levels) == iota((rows, members), 1))
    tall = lax.dot_general(repeat, weights.astype(BF16), NT, preferred_element_type=F32).astype(BF16)
    shares, _, cols = mix0_ref.shape
    i = iota((rows, cols), 0)
    j = iota((rows, cols), 1)
    level = i - quotient(i, levels) * levels
    in_rest = j < other * local
    same = jnp.logical_and(in_rest, level == j - quotient(j, other) * other + 1)
    zero = jnp.logical_and(j >= gap, level == 0)
    k = iota((members, cols), 0)
    j = iota((members, cols), 1)
    for c, ref in enumerate((mix0_ref, mix1_ref)):
        offset = gap + c * local
        ours = jnp.where(j < other * local, quotient(j, other), jnp.where(j >= offset, j - offset, -members))
        ours = jnp.where(jnp.logical_and(ours >= 0, ours < local), ours, -members)
        for s in range(shares):
            widen = ones_where(k == ours + (s ^ z) * local)
            wide = jnp.dot(tall, widen, preferred_element_type=F32)
            ref[s] = jnp.where(jnp.logical_or(same, zero), wide, 0.0).astype(BF16)
    i = iota((2 * members, members), 0)
    repeat = ones_where(member_of(i, 2) == iota((2 * members, members), 1), F32)
    tall = lax.dot_general(repeat, weights, NT, precision=HIGHEST, preferred_element_type=F32)
    odd = i - 2 * quotient(i, 2) == 1
    pos_ref[:, :members] = jnp.where(odd, 0.0, tall)
    pos_ref[:, members:] = jnp.where(odd, tall, 0.0)


def mix_sizes(local, levels):
    gap = round_up(local * (levels - 1), 16)
    return gap, round_up(gap + 2 * local, 16)


def spread_weights(z, weights, local, levels):
    members = weights.shape[0]
    rows = members * levels
    gap, cols = mix_sizes(local, levels)
    return pl.pallas_call(
        functools.partial(spread_kernel, members, local, levels, gap),
        in_specs=[smem(), vmem()],
        out_specs=[vmem()] * 3,
        out_shape=[
            jax.ShapeDtypeStruct((members // local, rows, cols), BF16),
            jax.ShapeDtypeStruct((members // local, rows, cols), BF16),
            jax.ShapeDtypeStruct((2 * members, 2 * members), F32),
        ],
        name="spread",
    )(z, weights)


def mix_kernel(shares, gap, w_ref, *refs):
    rest_refs, zero_refs, out_refs, both_ref = refs[:shares], refs[shares : 2 * shares], refs[2 * shares : -1], refs[-1]
    rest_rows, share = rest_refs[0].shape
    zero_rows = zero_refs[0].shape[0]
    both_ref[...] = jnp.zeros_like(both_ref)
    for s in range(shares):
        both_ref[s, :rest_rows, :] = rest_refs[s][...]
        both_ref[s, gap : gap + zero_rows, :] = zero_refs[s][:, :share]
    rows = out_refs[0].shape[0]
    for r in range(shares):
        total = jnp.zeros((rows, share), F32)
        for s in range(shares):
            total += jnp.dot(w_ref[s, r * rows : (r + 1) * rows, :], both_ref[s], preferred_element_type=F32)
        out_refs[r][...] = total.astype(BF16)


def mix(rest, zero, weights, local, levels):
    shares, rows, cols = weights.shape
    share = rest[0].shape[1]
    gap, _ = mix_sizes(local, levels)
    return pl.pallas_call(
        functools.partial(mix_kernel, shares, gap),
        in_specs=[vmem()] * (1 + 2 * shares),
        out_specs=[vmem()] * shares,
        out_shape=[jax.ShapeDtypeStruct((rows // shares, share), BF16)] * shares,
        scratch_shapes=[pltpu.VMEM((shares, cols, share), BF16)],
        name="mix",
    )(weights, *rest, *zero)


def join_kernel(shares, z_ref, *refs):
    out_ref = refs[-1]
    share = refs[0].shape[2]
    for r in range(shares):
        start = pl.multiple_of((z_ref[0] ^ r) * share, LANES)
        out_ref[:, 0, :, pl.ds(start, share)] = refs[r][...]


def join(z, pieces, comp, levels, earlier=None):
    shares = len(pieces)
    rows, share = pieces[0].shape
    local = rows // levels
    pieces = [p.reshape(local, levels, share) for p in pieces]
    more = [] if earlier is None else [earlier]
    return pl.pallas_call(
        functools.partial(join_kernel, shares),
        grid=(1,),
        in_specs=[smem()]
        + [pl.BlockSpec((local, levels, share), lambda n: (0, 0, 0))] * shares
        + [pl.BlockSpec(memory_space=pl.ANY)] * len(more),
        out_specs=pl.BlockSpec((local, 1, levels, shares * share), lambda n: (0, comp, 0, 0)),
        out_shape=jax.ShapeDtypeStruct((local, 2, levels, shares * share), BF16),
        input_output_aliases={1 + shares: 0} if more else {},
        name="join",
    )(z, *pieces, *more)


def move_kernel(pred_ref, req_ref, w_ref, out_ref):
    sources, _, _ = pred_ref.shape
    out_ref[...] = jnp.zeros_like(out_ref)

    def one_source(s, carry):
        amount = block_count(req_ref[s, 7:8, :])

        def one_block(b, c):
            lanes = pl.ds(pl.multiple_of(b * LANES, LANES), LANES)
            moved = jnp.dot(w_ref[...], pred_ref[s, :, lanes], precision=HIGHEST, preferred_element_type=F32)
            out_ref[s, :, lanes] = moved.astype(BF16)
            return c

        lax.fori_loop(0, amount, one_block, 0)
        return carry

    lax.fori_loop(0, sources, one_source, 0)


def move(pred, requests, w_pos):
    return pl.pallas_call(
        move_kernel,
        in_specs=[vmem()] * 3,
        out_specs=vmem(),
        out_shape=jax.ShapeDtypeStruct(pred.shape, BF16),
        name="move",
    )(pred, requests, w_pos)


def settle_kernel(back_ref, where_ref, count_ref, keep_ref, send_ref, acc_ref):
    tiles, _, capacity = back_ref.shape
    drifters = where_ref.shape[1]
    acc_ref[...] = jnp.zeros_like(acc_ref)
    where_to = where_ref[...]

    def one_tile(t, carry):
        amount = block_count(count_ref[pl.ds(t, 1), :])

        def one_block(b, c):
            lanes = pl.ds(pl.multiple_of(b * LANES, LANES), LANES)
            slot = iota((LANES, drifters), 0) + (t * capacity + b * LANES)
            hit = ones_where(slot == where_to)
            acc_ref[...] += jnp.dot(back_ref[t, :, lanes], hit, preferred_element_type=F32)
            return c

        lax.fori_loop(0, amount, one_block, 0)
        return carry

    lax.fori_loop(0, tiles, one_tile, 0)
    each = keep_ref.shape[1]
    for h in range(keep_ref.shape[0]):
        keep_ref[h] = acc_ref[2 * h * each : (2 * h + 1) * each, :].astype(BF16)
        send_ref[h] = acc_ref[(2 * h + 1) * each : (2 * h + 2) * each, :].astype(BF16)


def settle(back, where_to, count, shares):
    _, rows, _ = back.shape
    drifters = where_to.shape[1]
    return pl.pallas_call(
        settle_kernel,
        in_specs=[vmem()] * 3,
        out_specs=[vmem()] * 2,
        out_shape=[jax.ShapeDtypeStruct((shares // 2, rows // shares, drifters), BF16)] * 2,
        scratch_shapes=[pltpu.VMEM((rows, drifters), F32)],
        name="settle",
    )(back, where_to, count)


def exchange(x, axis):
    return lax.all_to_all(x, axis, split_axis=0, concat_axis=0, tiled=True)


def swap(x, axis, bits):
    return lax.ppermute(x, axis, [(n, n ^ bits) for n in range(lax.axis_size(axis))])


def trade(pieces, axis):
    got = [pieces[0]]
    for r in range(1, len(pieces)):
        got.append(swap(pieces[r], axis, r))
    return got


def after(pieces, other):
    return lax.optimization_barrier((pieces, other))[0]


def assimilate(velocity, start_frac, observed, obs_sd, tile_of, cell_of):
    local, _, levels, cells = velocity.shape
    drifters = cell_of.shape[0]
    tiles = lax.axis_size("tile")
    shares = lax.axis_size("mem")
    members = local * shares
    share = cells // shares
    blocks = pl.cdiv(2 * drifters // tiles, LANES)
    z = lax.axis_index("mem").astype(I32).reshape(1)

    zero, (rest0, rest1) = pack(z, velocity, shares)
    zero = trade(zero, "mem")
    requests, where_to, count = route(z, tile_of, cell_of, start_frac, observed, obs_sd, tiles, blocks, share)
    requests = exchange(requests, "tile")
    rest0 = trade(rest0, "mem")
    pred, gram = observe(z, zero, requests, members, local)
    gram = all_sum(gram)
    rest1 = trade(after(rest1, gram), "mem")
    weights = ensemble_weights(gram[:, :members], gram[:, members])
    w_mix0, w_mix1, w_pos = spread_weights(z, weights, local, levels)

    mixed0 = trade(mix(rest0, zero, w_mix0, local, levels), "mem")
    mixed1 = trade(mix(rest1, zero, w_mix1, local, levels), "mem")
    moved = exchange(move(pred, requests, w_pos), "tile")
    keep, send = settle(moved, where_to, count, shares)
    settled = keep + swap(send, "mem", 1)
    bits = 2
    while bits < shares:
        settled = settled[0::2] + swap(settled[1::2], "mem", bits)
        bits *= 2
    new_positions = settled[0].astype(F32).reshape(local, 2, drifters)
    new_velocity = join(z, mixed0, 0, levels)
    new_velocity = join(z, mixed1, 1, levels, new_velocity)
    return new_velocity, new_positions


def solution(mesh):
    in_specs = (
        P("mem", None, None, "tile"),
        P(None, "tile"),
        P(None, "tile"),
        P("tile"),
        P("tile", None),
        P("tile"),
    )
    out_specs = (P("mem", None, None, "tile"), P("mem", None, "tile"))
    return jax.shard_map(assimilate, mesh=mesh, in_specs=in_specs, out_specs=out_specs, check_vma=False)
```

time: 272 us -> 256 us (0.941)
  blocking collectives: 43.5 us -> 0 us
  starting transfers between devices: 35.3 us -> 56 us
  Pallas kernels: 52.3 us -> 59 us
  local copies, waits for them, and re-layouts: 4.44 us -> 7.29 us
    all_to_all x6 -> x2, waiting for transfers between devices: 109 us -> 0.01 us  [exchange(): return lax.all_to_all(x, axis, split_axis=0, concat_axis=0, tiled=True)]
    ppermute x0 -> x17, waiting for transfers between devices: none -> 105 us  [swap(): lax.ppermute(x, axis, [(n, n ^ bits) for n in range(lax.axis_size(axis))])]
    all_to_all x2 -> x0, blocking collectives: 43.5 us -> none  [exchange(): return lax.all_to_all(x, axis, split_axis=0, concat_axis=0, tiled=True)]
    ppermute x0 -> x17, starting transfers between devices: none -> 34.5 us  [swap(): lax.ppermute(x, axis, [(n, n ^ bits) for n in range(lax.axis_size(axis))])]
    all_to_all x6 -> x2, starting transfers between devices: 23.1 us -> 8.96 us  [exchange(): return lax.all_to_all(x, axis, split_axis=0, concat_axis=0, tiled=True)]
    pallas_call x6 -> x9, Pallas kernels: 28.5 us -> 34.7 us  [the longest x3 10.4 us: call(): pl.pallas_call(kernel, in_specs=[smem(), vmem()], out_specs=[vmem()] * sh...]
    ppermute x6, waiting for transfers between devices: 3.47 us -> 6.98 us  [all_sum(): lax.ppermute(x, axis, [(n, n ^ bit * k) for n in range(size)])]
    unnamed x12 -> x36, local copies, waits for them, and re-layouts: 3.21 us -> 6.04 us
  transfers between devices with their start and end apart: 13 -> 26, of which waited for: 9 -> 13; matrix products, arithmetic and copies ran while one was open for 8% -> 0% of each run, Pallas kernels for 11% -> 12%
where the time goes in v1:
time: 256 us
  waiting for transfers between devices  113 us (44%)
  Pallas kernels  59 us (23%)
  starting transfers between devices  56 us (22%)
  other arithmetic  19.1 us (7%)
  local copies, waits for them, and re-layouts  7.29 us (3%)
    ppermute x17, waiting for transfers between devices, swap(): lax.ppermute(x, axis, [(n, n ^ bits) for n in range(lax.axis_size(axis))])  105 us
    ppermute x17, starting transfers between devices, swap(): lax.ppermute(x, axis, [(n, n ^ bits) for n in range(lax.axis_size(axis))])  34.5 us
    pallas_call x1, Pallas kernels, observe(): pl.pallas_call(functools.partial(observe_kernel, members, local), in_spec...  13.9 us
    ppermute x6, starting transfers between devices, all_sum(): lax.ppermute(x, axis, [(n, n ^ bit * k) for n in range(size)])  12.5 us
    pallas_call x3, Pallas kernels, call(): pl.pallas_call(kernel, in_specs=[smem(), vmem()], out_specs=[vmem()] * sh...  10.4 us
    another operation x3, other arithmetic, ensemble_weights(): factor = jnp.linalg.cholesky(identity + gram_matrix)  9.45 us
    all_to_all x2, starting transfers between devices, exchange(): return lax.all_to_all(x, axis, split_axis=0, concat_axis=0, tiled=True)  8.96 us
    pallas_call x2, Pallas kernels, mix(): pl.pallas_call(functools.partial(mix_kernel, shares, gap), in_specs=[vmem...  8.9 us
  transfers between devices with their start and end apart: 26, of which 13 were waited for; matrix products, arithmetic and copies ran while one was open for 0% of the time, Pallas kernels for 12%

profile of v1, /device:TPU:0, one launch (start us, length us, event | category | flops | bytes accessed | tf_op | source)
XLA Modules:
  0.0 255.7 jit_solution(10612212233681822019)
XLA Ops:
  0.6 3.6 %route.1 = (f32[8,32,128]{2,1,0:T(8,128)}, s32[1,2048]{1,0:T(1,128)}, f32[8,128]{1,0:T(8,128)}) custom-call(s32[1]{0:T(128)} %bitcast.q_ref.z_ref, s32[1,2048]{1,0:T(1,128)} %bitcast.48, s32[1,2048]{1,0:T(1,128)} %bitcast.49, f32[2,2048]{1,0:T(2,128)} %frac_ref.1, f32[2,2048]{1,0:T(2,128)} %obs_ref.1, f32[1,2048]{1,0:T(1,128)} %bitcast.50), custom_call_target="tpu_custom_call" | custom-call | tf_op jit(solution)/shard_map/route/pallas_call | solution.py:127
  4.2 5.2 %all-to-all-start = ((f32[8,32,128]{2,1,0:T(8,128)}), f32[8,32,128]{2,1,0:T(8,128)S(1)}, u32[]{:S(2)}, u32[]{:S(2)}) async-start(f32[8,32,128]{2,1,0:T(8,128)} %get-tuple-element.36), calls=%async_computation | async-start | bytes 262144 | tf_op jit(solution)/shard_map/all_to_all | solution.py:439
  9.4 3.3 %shard_map.77 = (bf16[48,1152]{1,0:T(8,128)(2,1)}, bf16[48,1152]{1,0:T(8,128)(2,1)}, bf16[48,1152]{1,0:T(8,128)(2,1)}, bf16[48,1152]{1,0:T(8,128)(2,1)}) custom-call(s32[1]{0:T(128)} %bitcast.q_ref.z_ref, bf16[384,4096]{1,0:T(8,128)(2,1)} %bitcast.37), custom_call_target="tpu_custom_call" | custom-call | tf_op jit(solution)/shard_map/pallas_call | solution.py:81
  12.7 1.6 collective-permute-start
  14.3 2.6 %collective-permute-start.1 = (bf16[48,1152]{1,0:T(8,128)(2,1)}, bf16[48,1152]{1,0:T(8,128)(2,1)S(1)}, u32[]{:S(2)}, u32[]{:S(2)}) collective-permute-start(bf16[48,1152]{1,0:T(8,128)(2,1)} %get-tuple-element.39), channel_id=1, source_target_pairs={{0,2},{1,3},{2,0},{3,1},{4,6},{5,7},{6,4},{7,5},{8,10},{9,11},{10,... | collective-permute-start | bytes 331784 | tf_op jit(solution)/shard_map/ppermute | solution.py:443
  16.9 0.2 collective-permute-start.2
  17.1 3.0 %collective-permute-done.refs_1_.refs_5_ = bf16[48,1152]{1,0:T(8,128)(2,1)S(1)} collective-permute-done((bf16[48,1152]{1,0:T(8,128)(2,1)}, bf16[48,1152]{1,0:T(8,128)(2,1)S(1)}, u32[]{:S(2)}, u32[]{:S(2)}) %collective-permute-start) | collective-permute-done | bytes 110624 | tf_op jit(solution)/shard_map/ppermute | solution.py:443
  20.1 6.0 %collective-permute-done.1.refs_2_.refs_6_ = bf16[48,1152]{1,0:T(8,128)(2,1)S(1)} collective-permute-done((bf16[48,1152]{1,0:T(8,128)(2,1)}, bf16[48,1152]{1,0:T(8,128)(2,1)S(1)}, u32[]{:S(2)}, u32[]{:S(2)}) %collective-permute-start.1) | collective-permute-done | bytes 110624 | tf_op jit(solution)/shard_map/ppermute | solution.py:443
  26.2 0.6 copy-done.3
  26.9 13.9 %observe.1 = (f32[8,192,512]{2,1,0:T(8,128)}, f32[96,128]{1,0:T(8,128)}) custom-call(s32[1]{0:T(128)} %bitcast.q_ref.z_ref, f32[8,32,128]{2,1,0:T(8,128)} %copy-done.1, bf16[48,1152]{1,0:T(8,128)(2,1)} %get-tuple-element.37.refs_0_.refs_4_, bf16[48,1152]{1,0:T(8,128)(2,1)} %copy-done.2, bf16[48,1152]{1,0:T(8,128)(2,1)} %copy-done.3, bf16[48,1152]{1,0:T(8,128)(2,1)} %copy-done.4), custom_call_target="tpu_custom_call" | custom-call | tf_op jit(solution)/shard_map/observe/pallas_call | solution.py:213
  40.8 1.4 collective-permute-done.3
  42.2 0.8 add.59
  43.0 6.5 %collective-permute-start.4 = (f32[96,128]{1,0:T(8,128)S(1)}, f32[96,128]{1,0:T(8,128)S(1)}, u32[]{:S(2)}, u32[]{:S(2)}) collective-permute-start(f32[96,128]{1,0:T(8,128)S(1)} %add.59), channel_id=1, source_target_pairs={{0,8},{4,12},{8,0},{12,4},{16,24},{20,28},{24,16},{28,20},{1,9},{5... | collective-permute-start | bytes 147464 | tf_op jit(solution)/shard_map/ppermute | solution.py:232
  49.5 1.5 collective-permute-start.6
  51.0 0.7 collective-permute-done.4
  51.8 2.9 %collective-permute-done.5 = f32[96,128]{1,0:T(8,128)S(1)} collective-permute-done((f32[96,128]{1,0:T(8,128)S(1)}, f32[96,128]{1,0:T(8,128)S(1)}, u32[]{:S(2)}, u32[]{:S(2)}) %collective-permute-start.5) | collective-permute-done | bytes 49184 | tf_op jit(solution)/shard_map/ppermute | solution.py:232
  54.7 1.8 collective-permute-start.7
  56.5 2.6 %collective-permute-start.9 = (f32[96,128]{1,0:T(8,128)S(1)}, f32[96,128]{1,0:T(8,128)S(1)}, u32[]{:S(2)}, u32[]{:S(2)}) collective-permute-start(f32[96,128]{1,0:T(8,128)S(1)} %add_add_fusion.1), channel_id=1, source_target_pairs={{0,3},{1,2},{2,1},{3,0},{4,7},{5,6},{6,5},{7,4},{8,11},{9,10},{10,... | collective-permute-start | bytes 147464 | tf_op jit(solution)/shard_map/ppermute | solution.py:232
  59.1 2.6 %collective-permute-done.8 = f32[96,128]{1,0:T(8,128)S(1)} collective-permute-done((f32[96,128]{1,0:T(8,128)S(1)}, f32[96,128]{1,0:T(8,128)S(1)}, u32[]{:S(2)}, u32[]{:S(2)}) %collective-permute-start.8) | collective-permute-done | bytes 49184 | tf_op jit(solution)/shard_map/ppermute | solution.py:232
  61.7 0.8 collective-permute-done.9
  62.5 0.2 slice_reduce_fusion
  62.8 8.8 %cholesky.18 = f32[96,96]{1,0:T(8,128)S(1)} custom-call(f32[96,96]{1,0:T(8,128)S(1)} %fusion.6), custom_call_target="Cholesky" | custom-call | tf_op jit(solution)/shard_map/jit(cholesky)/cholesky | solution.py:244
  71.6 0.6 compare_reduce_fusion
  72.3 0.7 fusion.2
  72.9 7.4 %custom-call.10 = f32[1,96,96]{1,2,0:T(8,128)S(1)} custom-call(f32[1,96,96]{2,1,0:T(8,128)S(1)} %fusion.2), custom_call_target="InvertDiagBlocksLowerTriangular" | custom-call | tf_op jit(solution)/shard_map/triangular_solve | solution.py:246
  80.3 0.1 convolution_bitcast_fusion.1
  80.5 0.2 convolution_bitcast_fusion
  80.6 0.2 fusion.8
  80.9 0.6 subtract_add_fusion.w_ref
  81.5 3.5 %spread.1 = (bf16[4,768,224]{2,1,0:T(8,128)(2,1)}, bf16[4,768,224]{2,1,0:T(8,128)(2,1)}, f32[192,192]{1,0:T(8,128)}) custom-call(s32[1]{0:T(128)} %bitcast.q_ref.z_ref, f32[96,96]{1,0:T(8,128)} %subtract_add_fusion.w_ref), custom_call_target="tpu_custom_call" | custom-call | tf_op jit(solution)/shard_map/spread/pallas_call | solution.py:300
  85.0 6.8 %move.1 = bf16[8,192,512]{2,1,0:T(8,128)(2,1)} custom-call(f32[8,192,512]{2,1,0:T(8,128)} %get-tuple-element.64.pred_ref, f32[8,32,128]{2,1,0:T(8,128)} %copy-done.1, f32[192,192]{1,0:T(8,128)} %get-tuple-element.65.w_ref), custom_call_target="tpu_custom_call" | custom-call | tf_op jit(solution)/shard_map/move/pallas_call | solution.py:390
  91.7 3.8 %all-to-all-start.1 = ((bf16[8,192,512]{2,1,0:T(8,128)(2,1)}), bf16[8,192,512]{2,1,0:T(8,128)(2,1)S(1)}, u32[]{:S(2)}, u32[]{:S(2)}) async-start(bf16[8,192,512]{2,1,0:T(8,128)(2,1)} %move.1), calls=%async_computation.1 | async-start | bytes 3145728 | tf_op jit(solution)/shard_map/all_to_all | solution.py:439
  95.5 3.6 %shard_map.79 = (bf16[168,1024]{1,0:T(8,128)(2,1)}, bf16[168,1024]{1,0:T(8,128)(2,1)}, bf16[168,1024]{1,0:T(8,128)(2,1)}, bf16[168,1024]{1,0:T(8,128)(2,1)}) custom-call(s32[1]{0:T(128)} %bitcast.q_ref.z_ref, bf16[384,4096]{1,0:T(8,128)(2,1)} %bitcast.38), custom_call_target="tpu_custom_call" | custom-call | tf_op jit(solution)/shard_map/pallas_call | solution.py:81
  99.1 0.8 collective-permute-start.16
  99.9 2.2 collective-permute-start.17
  102.2 1.3 collective-permute-start.18
  103.5 3.6 %shard_map.78 = (bf16[168,1024]{1,0:T(8,128)(2,1)}, bf16[168,1024]{1,0:T(8,128)(2,1)}, bf16[168,1024]{1,0:T(8,128)(2,1)}, bf16[168,1024]{1,0:T(8,128)(2,1)}) custom-call(s32[1]{0:T(128)} %bitcast.q_ref.z_ref, bf16[384,4096]{1,0:T(8,128)(2,1)} %bitcast.39), custom_call_target="tpu_custom_call" | custom-call | tf_op jit(solution)/shard_map/pallas_call | solution.py:81
  107.0 9.8 %collective-permute-done.16.refs_1_ = bf16[168,1024]{1,0:T(8,128)(2,1)S(1)} collective-permute-done((bf16[168,1024]{1,0:T(8,128)(2,1)}, bf16[168,1024]{1,0:T(8,128)(2,1)S(1)}, u32[]{:S(2)}, u32[]{:S(2)}) %collective-permute-start.16) | collective-permute-done | bytes 344096 | tf_op jit(solution)/shard_map/ppermute | solution.py:443
  116.8 10.0 %collective-permute-done.17.refs_2_ = bf16[168,1024]{1,0:T(8,128)(2,1)S(1)} collective-permute-done((bf16[168,1024]{1,0:T(8,128)(2,1)}, bf16[168,1024]{1,0:T(8,128)(2,1)S(1)}, u32[]{:S(2)}, u32[]{:S(2)}) %collective-permute-start.17) | collective-permute-done | bytes 344096 | tf_op jit(solution)/shard_map/ppermute | solution.py:443
  126.8 0.8 copy-done.15
  127.5 0.1 copy-done.17
  127.7 4.4 %mix.3 = (bf16[192,1024]{1,0:T(8,128)(2,1)}, bf16[192,1024]{1,0:T(8,128)(2,1)}, bf16[192,1024]{1,0:T(8,128)(2,1)}, bf16[192,1024]{1,0:T(8,128)(2,1)}) custom-call(bf16[4,768,224]{2,1,0:T(8,128)(2,1)} %get-tuple-element.55.w_ref, bf16[168,1024]{1,0:T(8,128)(2,1)} %get-tuple-element.56.refs_0_, bf16[168,1024]{1,0:T(8,128)(2,1)} %copy-done.13, ...), custom_call_target="tpu_custom_call" | custom-call | tf_op jit(solution)/shard_map/mix/pallas_call | solution.py:333
  132.1 6.8 %collective-permute-start.19 = (bf16[192,1024]{1,0:T(8,128)(2,1)}, bf16[192,1024]{1,0:T(8,128)(2,1)S(1)}, u32[]{:S(2)}, u32[]{:S(2)}) collective-permute-start(bf16[192,1024]{1,0:T(8,128)(2,1)} %get-tuple-element.61), channel_id=1, source_target_pairs={{0,1},{1,0},{2,3},{3,2},{4,5},{5,4},{6,7},{7,6},{8,9},{9,8},{10,11... | collective-permute-start | bytes 1179656 | tf_op jit(solution)/shard_map/ppermute | solution.py:443
  138.9 1.1 copy-done
  140.0 6.7 %settle.1 = (bf16[2,48,2048]{2,1,0:T(8,128)(2,1)}, bf16[2,48,2048]{2,1,0:T(8,128)(2,1)}) custom-call(bf16[8,192,512]{2,1,0:T(8,128)(2,1)} %copy-done, s32[1,2048]{1,0:T(1,128)} %get-tuple-element.66.where_ref, f32[8,128]{1,0:T(8,128)} %get-tuple-element.67.count_ref), custom_call_target="tpu_custom_call" | custom-call | tf_op jit(solution)/shard_map/settle/pallas_call | solution.py:428
  146.8 2.5 collective-permute-start.11
  149.3 1.9 collective-permute-start.12
  151.1 0.7 copy-done.12
  151.9 34.3 %collective-permute-done.11.refs_2_ = bf16[168,1024]{1,0:T(8,128)(2,1)S(1)} collective-permute-done((bf16[168,1024]{1,0:T(8,128)(2,1)}, bf16[168,1024]{1,0:T(8,128)(2,1)S(1)}, u32[]{:S(2)}, u32[]{:S(2)}) %collective-permute-start.11) | collective-permute-done | bytes 344096 | tf_op jit(solution)/shard_map/ppermute | solution.py:443
  186.2 2.0 collective-permute-start.21
  188.2 0.7 copy-done.16
  188.9 4.5 %mix.2 = (bf16[192,1024]{1,0:T(8,128)(2,1)}, bf16[192,1024]{1,0:T(8,128)(2,1)}, bf16[192,1024]{1,0:T(8,128)(2,1)}, bf16[192,1024]{1,0:T(8,128)(2,1)}) custom-call(bf16[4,768,224]{2,1,0:T(8,128)(2,1)} %get-tuple-element.42.w_ref, bf16[168,1024]{1,0:T(8,128)(2,1)} %get-tuple-element.47.refs_0_, bf16[168,1024]{1,0:T(8,128)(2,1)} %copy-done.12, ...), custom_call_target="tpu_custom_call" | custom-call | tf_op jit(solution)/shard_map/mix/pallas_call | solution.py:333
  193.4 10.2 %collective-permute-start.13 = (bf16[192,1024]{1,0:T(8,128)(2,1)}, bf16[192,1024]{1,0:T(8,128)(2,1)S(1)}, u32[]{:S(2)}, u32[]{:S(2)}) collective-permute-start(bf16[192,1024]{1,0:T(8,128)(2,1)} %get-tuple-element.52), channel_id=1, source_target_pairs={{0,1},{1,0},{2,3},{3,2},{4,5},{5,4},{6,7},{7,6},{8,9},{9,8},{10,11... | collective-permute-start | bytes 1179656 | tf_op jit(solution)/shard_map/ppermute | solution.py:443
  203.5 0.6 collective-permute-start.14
  204.1 1.8 collective-permute-start.15
  206.1 8.1 %collective-permute-done.20 = bf16[192,1024]{1,0:T(8,128)(2,1)S(1)} collective-permute-done((bf16[192,1024]{1,0:T(8,128)(2,1)}, bf16[192,1024]{1,0:T(8,128)(2,1)S(1)}, u32[]{:S(2)}, u32[]{:S(2)}) %collective-permute-start.20) | collective-permute-done | bytes 393248 | tf_op jit(solution)/shard_map/ppermute | solution.py:443
  214.3 0.7 copy-done.9
  215.1 2.6 %join.2.refs_4_ = bf16[24,2,8,4096]{3,2,1,0:T(8,128)(2,1)} custom-call(s32[1]{0:T(128)} %bitcast.q_ref.z_ref, bf16[24,8,1024]{2,1,0:T(8,128)(2,1)} %bitcast.44, bf16[24,8,1024]{2,1,0:T(8,128)(2,1)} %bitcast.45, bf16[24,8,1024]{2,1,0:T(8,128)(2,1)} %bitcast.46, bf16[24,8,1024]{2,1,0:T(8,128)(2,1)} %bitcast.47), custom_call_target="tpu_custom_call" | custom-call | tf_op jit(solution)/shard_map/join/pallas_call | solution.py:357
  217.7 26.4 %collective-permute-done.14 = bf16[192,1024]{1,0:T(8,128)(2,1)S(1)} collective-permute-done((bf16[192,1024]{1,0:T(8,128)(2,1)}, bf16[192,1024]{1,0:T(8,128)(2,1)S(1)}, u32[]{:S(2)}, u32[]{:S(2)}) %collective-permute-start.14) | collective-permute-done | bytes 393248 | tf_op jit(solution)/shard_map/ppermute | solution.py:443
  244.2 0.8 copy-done.6
  244.9 0.1 copy-done.7
  245.1 2.6 %join.3 = bf16[24,2,8,4096]{3,2,1,0:T(8,128)(2,1)} custom-call(s32[1]{0:T(128)} %bitcast.q_ref.z_ref, bf16[24,8,1024]{2,1,0:T(8,128)(2,1)} %bitcast.40, bf16[24,8,1024]{2,1,0:T(8,128)(2,1)} %bitcast.41, bf16[24,8,1024]{2,1,0:T(8,128)(2,1)} %bitcast.42, bf16[24,8,1024]{2,1,0:T(8,128)(2,1)} %bitcast.43, ...), custom_call_target="tpu_custom_call", output_to_operand_aliasing={{}: (5, {})} | custom-call | tf_op jit(solution)/shard_map/join/pallas_call | solution.py:357
  247.7 7.1 %collective-permute-done.23 = bf16[1,48,2048]{2,1,0:T(8,128)(2,1)S(1)} collective-permute-done((bf16[1,48,2048]{2,1,0:T(8,128)(2,1)S(1)}, bf16[1,48,2048]{2,1,0:T(8,128)(2,1)S(1)}, u32[]{:S(2)}, u32[]{:S(2)}) %collective-permute-start.23) | collective-permute-done | bytes 196640 | tf_op jit(solution)/shard_map/ppermute | solution.py:443
  254.8 1.0 reshape.86
  (57 shorter events, 0.7 us)
Async XLA Ops:
  4.2 21.9 %all-to-all-start = ((f32[8,32,128]{2,1,0:T(8,128)}), f32[8,32,128]{2,1,0:T(8,128)S(1)}, u32[]{:S(2)}, u32[]{:S(2)}) async-start(f32[8,32,128]{2,1,0:T(8,128)} %get-tuple-element.36), calls=%async_computation | async-start | bytes 262144 | tf_op jit(solution)/shard_map/all_to_all | solution.py:439
  12.7 7.4 %collective-permute-start = (bf16[48,1152]{1,0:T(8,128)(2,1)}, bf16[48,1152]{1,0:T(8,128)(2,1)S(1)}, u32[]{:S(2)}, u32[]{:S(2)}) collective-permute-start(bf16[48,1152]{1,0:T(8,128)(2,1)} %get-tuple-element.38), channel_id=1, source_target_pairs={{0,1},{1,0},{2,3},{3,2},{4,5},{5,4},{6,7},{7,6},{8,9},{9,8},{10,11... | collective-permute-start | bytes 331784 | tf_op jit(solution)/shard_map/ppermute | solution.py:443
  14.3 11.8 %collective-permute-start.1 = (bf16[48,1152]{1,0:T(8,128)(2,1)}, bf16[48,1152]{1,0:T(8,128)(2,1)S(1)}, u32[]{:S(2)}, u32[]{:S(2)}) collective-permute-start(bf16[48,1152]{1,0:T(8,128)(2,1)} %get-tuple-element.39), channel_id=1, source_target_pairs={{0,2},{1,3},{2,0},{3,1},{4,6},{5,7},{6,4},{7,5},{8,10},{9,11},{10,... | collective-permute-start | bytes 331784 | tf_op jit(solution)/shard_map/ppermute | solution.py:443
  16.9 9.2 %collective-permute-start.2 = (bf16[48,1152]{1,0:T(8,128)(2,1)}, bf16[48,1152]{1,0:T(8,128)(2,1)S(1)}, u32[]{:S(2)}, u32[]{:S(2)}) collective-permute-start(bf16[48,1152]{1,0:T(8,128)(2,1)} %get-tuple-element.40), channel_id=1, source_target_pairs={{0,3},{1,2},{2,1},{3,0},{4,7},{5,6},{6,5},{7,4},{8,11},{9,10},{10,... | collective-permute-start | bytes 331784 | tf_op jit(solution)/shard_map/ppermute | solution.py:443
  20.1 6.1 %copy-start.2 = (bf16[48,1152]{1,0:T(8,128)(2,1)}, bf16[48,1152]{1,0:T(8,128)(2,1)S(1)}, u32[]{:S(2)}) copy-start(bf16[48,1152]{1,0:T(8,128)(2,1)S(1)} %collective-permute-done.refs_1_.refs_5_) | copy-start | bytes 331780
  26.1 0.7 copy-start.3
  26.1 0.7 copy-start.4
  26.1 0.7 copy-start.1
  40.8 1.4 collective-permute-start.3
  43.0 8.7 %collective-permute-start.4 = (f32[96,128]{1,0:T(8,128)S(1)}, f32[96,128]{1,0:T(8,128)S(1)}, u32[]{:S(2)}, u32[]{:S(2)}) collective-permute-start(f32[96,128]{1,0:T(8,128)S(1)} %add.59), channel_id=1, source_target_pairs={{0,8},{4,12},{8,0},{12,4},{16,24},{20,28},{24,16},{28,20},{1,9},{5... | collective-permute-start | bytes 147464 | tf_op jit(solution)/shard_map/ppermute | solution.py:232
  49.5 5.1 %collective-permute-start.5 = (f32[96,128]{1,0:T(8,128)S(1)}, f32[96,128]{1,0:T(8,128)S(1)}, u32[]{:S(2)}, u32[]{:S(2)}) collective-permute-start(f32[96,128]{1,0:T(8,128)S(1)} %add.59), channel_id=1, source_target_pairs={{0,16},{4,20},{8,24},{12,28},{16,0},{20,4},{24,8},{28,12},{1,17},{... | collective-permute-start | bytes 147464 | tf_op jit(solution)/shard_map/ppermute | solution.py:232
  49.5 5.1 %collective-permute-start.6 = (f32[96,128]{1,0:T(8,128)S(1)}, f32[96,128]{1,0:T(8,128)S(1)}, u32[]{:S(2)}, u32[]{:S(2)}) collective-permute-start(f32[96,128]{1,0:T(8,128)S(1)} %add.59), channel_id=1, source_target_pairs={{0,24},{4,28},{8,16},{12,20},{16,8},{20,12},{24,0},{28,4},{1,25},{... | collective-permute-start | bytes 147464 | tf_op jit(solution)/shard_map/ppermute | solution.py:232
  54.7 4.5 %collective-permute-start.7 = (f32[96,128]{1,0:T(8,128)S(1)}, f32[96,128]{1,0:T(8,128)S(1)}, u32[]{:S(2)}, u32[]{:S(2)}) collective-permute-start(f32[96,128]{1,0:T(8,128)S(1)} %add_add_fusion.1), channel_id=1, source_target_pairs={{0,1},{1,0},{2,3},{3,2},{4,5},{5,4},{6,7},{7,6},{8,9},{9,8},{10,11... | collective-permute-start | bytes 147464 | tf_op jit(solution)/shard_map/ppermute | solution.py:232
  56.5 5.2 %collective-permute-start.8 = (f32[96,128]{1,0:T(8,128)S(1)}, f32[96,128]{1,0:T(8,128)S(1)}, u32[]{:S(2)}, u32[]{:S(2)}) collective-permute-start(f32[96,128]{1,0:T(8,128)S(1)} %add_add_fusion.1), channel_id=1, source_target_pairs={{0,2},{1,3},{2,0},{3,1},{4,6},{5,7},{6,4},{7,5},{8,10},{9,11},{10,... | collective-permute-start | bytes 147464 | tf_op jit(solution)/shard_map/ppermute | solution.py:232
  56.5 6.0 %collective-permute-start.9 = (f32[96,128]{1,0:T(8,128)S(1)}, f32[96,128]{1,0:T(8,128)S(1)}, u32[]{:S(2)}, u32[]{:S(2)}) collective-permute-start(f32[96,128]{1,0:T(8,128)S(1)} %add_add_fusion.1), channel_id=1, source_target_pairs={{0,3},{1,2},{2,1},{3,0},{4,7},{5,6},{6,5},{7,4},{8,11},{9,10},{10,... | collective-permute-start | bytes 147464 | tf_op jit(solution)/shard_map/ppermute | solution.py:232
  91.7 47.2 %all-to-all-start.1 = ((bf16[8,192,512]{2,1,0:T(8,128)(2,1)}), bf16[8,192,512]{2,1,0:T(8,128)(2,1)S(1)}, u32[]{:S(2)}, u32[]{:S(2)}) async-start(bf16[8,192,512]{2,1,0:T(8,128)(2,1)} %move.1), calls=%async_computation.1 | async-start | bytes 3145728 | tf_op jit(solution)/shard_map/all_to_all | solution.py:439
  99.1 17.7 %collective-permute-start.16 = (bf16[168,1024]{1,0:T(8,128)(2,1)}, bf16[168,1024]{1,0:T(8,128)(2,1)S(1)}, u32[]{:S(2)}, u32[]{:S(2)}) collective-permute-start(bf16[168,1024]{1,0:T(8,128)(2,1)} %get-tuple-element.57), channel_id=1, source_target_pairs={{0,1},{1,0},{2,3},{3,2},{4,5},{5,4},{6,7},{7,6},{8,9},{9,8},{10,11... | collective-permute-start | bytes 1032200 | tf_op jit(solution)/shard_map/ppermute | solution.py:443
  99.9 26.8 %collective-permute-start.17 = (bf16[168,1024]{1,0:T(8,128)(2,1)}, bf16[168,1024]{1,0:T(8,128)(2,1)S(1)}, u32[]{:S(2)}, u32[]{:S(2)}) collective-permute-start(bf16[168,1024]{1,0:T(8,128)(2,1)} %get-tuple-element.58), channel_id=1, source_target_pairs={{0,2},{1,3},{2,0},{3,1},{4,6},{5,7},{6,4},{7,5},{8,10},{9,11},{10,... | collective-permute-start | bytes 1032200 | tf_op jit(solution)/shard_map/ppermute | solution.py:443
  102.2 24.6 %collective-permute-start.18 = (bf16[168,1024]{1,0:T(8,128)(2,1)}, bf16[168,1024]{1,0:T(8,128)(2,1)S(1)}, u32[]{:S(2)}, u32[]{:S(2)}) collective-permute-start(bf16[168,1024]{1,0:T(8,128)(2,1)} %get-tuple-element.59), channel_id=1, source_target_pairs={{0,3},{1,2},{2,1},{3,0},{4,7},{5,6},{6,5},{7,4},{8,11},{9,10},{10,... | collective-permute-start | bytes 1032200 | tf_op jit(solution)/shard_map/ppermute | solution.py:443
  107.0 44.1 %collective-permute-start.10 = (bf16[168,1024]{1,0:T(8,128)(2,1)}, bf16[168,1024]{1,0:T(8,128)(2,1)S(1)}, u32[]{:S(2)}, u32[]{:S(2)}) collective-permute-start(bf16[168,1024]{1,0:T(8,128)(2,1)} %get-tuple-element.48), channel_id=1, source_target_pairs={{0,1},{1,0},{2,3},{3,2},{4,5},{5,4},{6,7},{7,6},{8,9},{9,8},{10,11... | collective-permute-start | bytes 1032200 | tf_op jit(solution)/shard_map/ppermute | solution.py:443
  116.8 10.0 %copy-start.13 = (bf16[168,1024]{1,0:T(8,128)(2,1)}, bf16[168,1024]{1,0:T(8,128)(2,1)S(1)}, u32[]{:S(2)}) copy-start(bf16[168,1024]{1,0:T(8,128)(2,1)S(1)} %collective-permute-done.16.refs_1_) | copy-start | bytes 1032196
  126.8 0.8 copy-start.15
  126.8 0.9 copy-start.17
  132.1 71.4 %collective-permute-start.19 = (bf16[192,1024]{1,0:T(8,128)(2,1)}, bf16[192,1024]{1,0:T(8,128)(2,1)S(1)}, u32[]{:S(2)}, u32[]{:S(2)}) collective-permute-start(bf16[192,1024]{1,0:T(8,128)(2,1)} %get-tuple-element.61), channel_id=1, source_target_pairs={{0,1},{1,0},{2,3},{3,2},{4,5},{5,4},{6,7},{7,6},{8,9},{9,8},{10,11... | collective-permute-start | bytes 1179656 | tf_op jit(solution)/shard_map/ppermute | solution.py:443
  138.9 1.1 copy-start
  146.7 59.2 %copy-start.11 = (bf16[2,48,2048]{2,1,0:T(8,128)(2,1)S(1)}, bf16[2,48,2048]{2,1,0:T(8,128)(2,1)}, u32[]{:S(2)}) copy-start(bf16[2,48,2048]{2,1,0:T(8,128)(2,1)} %get-tuple-element.68) | copy-start | bytes 1179652
  146.7 57.4 %collective-permute-start.22 = (bf16[2,48,2048]{2,1,0:T(8,128)(2,1)}, bf16[2,48,2048]{2,1,0:T(8,128)(2,1)S(1)}, u32[]{:S(2)}, u32[]{:S(2)}) collective-permute-start(bf16[2,48,2048]{2,1,0:T(8,128)(2,1)} %get-tuple-element.69), channel_id=1, source_target_pairs={{0,1},{1,0},{2,3},{3,2},{4,5},{5,4},{6,7},{7,6},{8,9},{9,8},{10,11... | collective-permute-start | bytes 1179656 | tf_op jit(solution)/shard_map/ppermute | solution.py:443
  146.8 39.4 %collective-permute-start.11 = (bf16[168,1024]{1,0:T(8,128)(2,1)}, bf16[168,1024]{1,0:T(8,128)(2,1)S(1)}, u32[]{:S(2)}, u32[]{:S(2)}) collective-permute-start(bf16[168,1024]{1,0:T(8,128)(2,1)} %get-tuple-element.49), channel_id=1, source_target_pairs={{0,2},{1,3},{2,0},{3,1},{4,6},{5,7},{6,4},{7,5},{8,10},{9,11},{10,... | collective-permute-start | bytes 1032200 | tf_op jit(solution)/shard_map/ppermute | solution.py:443
  149.3 38.9 %collective-permute-start.12 = (bf16[168,1024]{1,0:T(8,128)(2,1)}, bf16[168,1024]{1,0:T(8,128)(2,1)S(1)}, u32[]{:S(2)}, u32[]{:S(2)}) collective-permute-start(bf16[168,1024]{1,0:T(8,128)(2,1)} %get-tuple-element.50), channel_id=1, source_target_pairs={{0,3},{1,2},{2,1},{3,0},{4,7},{5,6},{6,5},{7,4},{8,11},{9,10},{10,... | collective-permute-start | bytes 1032200 | tf_op jit(solution)/shard_map/ppermute | solution.py:443
  151.1 0.7 copy-start.12
  151.9 62.4 %collective-permute-start.20 = (bf16[192,1024]{1,0:T(8,128)(2,1)}, bf16[192,1024]{1,0:T(8,128)(2,1)S(1)}, u32[]{:S(2)}, u32[]{:S(2)}) collective-permute-start(bf16[192,1024]{1,0:T(8,128)(2,1)} %get-tuple-element.62), channel_id=1, source_target_pairs={{0,2},{1,3},{2,0},{3,1},{4,6},{5,7},{6,4},{7,5},{8,10},{9,11},{10,... | collective-permute-start | bytes 1179656 | tf_op jit(solution)/shard_map/ppermute | solution.py:443
  186.2 2.0 copy-start.14
  186.2 28.1 %collective-permute-start.21 = (bf16[192,1024]{1,0:T(8,128)(2,1)}, bf16[192,1024]{1,0:T(8,128)(2,1)S(1)}, u32[]{:S(2)}, u32[]{:S(2)}) collective-permute-start(bf16[192,1024]{1,0:T(8,128)(2,1)} %get-tuple-element.63), channel_id=1, source_target_pairs={{0,3},{1,2},{2,1},{3,0},{4,7},{5,6},{6,5},{7,4},{8,11},{9,10},{10,... | collective-permute-start | bytes 1179656 | tf_op jit(solution)/shard_map/ppermute | solution.py:443
  188.2 0.7 copy-start.16
  193.4 24.4 %collective-permute-start.13 = (bf16[192,1024]{1,0:T(8,128)(2,1)}, bf16[192,1024]{1,0:T(8,128)(2,1)S(1)}, u32[]{:S(2)}, u32[]{:S(2)}) collective-permute-start(bf16[192,1024]{1,0:T(8,128)(2,1)} %get-tuple-element.52), channel_id=1, source_target_pairs={{0,1},{1,0},{2,3},{3,2},{4,5},{5,4},{6,7},{7,6},{8,9},{9,8},{10,11... | collective-permute-start | bytes 1179656 | tf_op jit(solution)/shard_map/ppermute | solution.py:443
  203.5 10.7 %copy-start.8 = (bf16[192,1024]{1,0:T(8,128)(2,1)}, bf16[192,1024]{1,0:T(8,128)(2,1)S(1)}, u32[]{:S(2)}) copy-start(bf16[192,1024]{1,0:T(8,128)(2,1)S(1)} %collective-permute-done.19) | copy-start | bytes 1179652
  203.5 40.6 %collective-permute-start.14 = (bf16[192,1024]{1,0:T(8,128)(2,1)}, bf16[192,1024]{1,0:T(8,128)(2,1)S(1)}, u32[]{:S(2)}, u32[]{:S(2)}) collective-permute-start(bf16[192,1024]{1,0:T(8,128)(2,1)} %get-tuple-element.53), channel_id=1, source_target_pairs={{0,2},{1,3},{2,0},{3,1},{4,6},{5,7},{6,4},{7,5},{8,10},{9,11},{10,... | collective-permute-start | bytes 1179656 | tf_op jit(solution)/shard_map/ppermute | solution.py:443
  204.1 40.0 %collective-permute-start.15 = (bf16[192,1024]{1,0:T(8,128)(2,1)}, bf16[192,1024]{1,0:T(8,128)(2,1)S(1)}, u32[]{:S(2)}, u32[]{:S(2)}) collective-permute-start(bf16[192,1024]{1,0:T(8,128)(2,1)} %get-tuple-element.54), channel_id=1, source_target_pairs={{0,3},{1,2},{2,1},{3,0},{4,7},{5,6},{6,5},{7,4},{8,11},{9,10},{10,... | collective-permute-start | bytes 1179656 | tf_op jit(solution)/shard_map/ppermute | solution.py:443
  214.2 0.8 copy-start.9
  214.2 40.5 %collective-permute-start.23 = (bf16[1,48,2048]{2,1,0:T(8,128)(2,1)S(1)}, bf16[1,48,2048]{2,1,0:T(8,128)(2,1)S(1)}, u32[]{:S(2)}, u32[]{:S(2)}) collective-permute-start(bf16[1,48,2048]{2,1,0:T(8,128)(2,1)S(1)} %slice.36), channel_id=1, source_target_pairs={{0,2},{1,3},{2,0},{3,1},{4,6},{5,7},{6,4},{7,5},{8,10},{9,11},{10,... | collective-permute-start | bytes 589832 | tf_op jit(solution)/shard_map/ppermute | solution.py:443
  214.2 0.9 copy-start.10
  217.7 26.4 %copy-start.5 = (bf16[192,1024]{1,0:T(8,128)(2,1)}, bf16[192,1024]{1,0:T(8,128)(2,1)S(1)}, u32[]{:S(2)}) copy-start(bf16[192,1024]{1,0:T(8,128)(2,1)S(1)} %collective-permute-done.13) | copy-start | bytes 1179652
  244.2 0.8 copy-start.6
  244.2 0.9 copy-start.7

commit v2 on v1

--- a/solution.py
+++ b/solution.py
@@ -17,6 +17,7 @@
 I32 = jnp.int32
 HIGHEST = lax.Precision.HIGHEST
 NT = (((1,), (1,)), ((), ()))
+TN = (((0,), (0,)), ((), ()))
 
 
 def iota(shape, dim):
@@ -171,40 +172,45 @@
     spread = math.sqrt(members - 1)
 
     def one_block(s, b):
-        r = req_ref[s, pl.ds(pl.multiple_of(b * 8, 8), 8), :]
-        cell = r[0:1].astype(I32)
-        hit = ones_where(iota((width, LANES), 0) == cell)
+        rows_of = pl.ds(pl.multiple_of(b * 8, 8), 8)
+        lanes = pl.ds(pl.multiple_of(b * LANES, LANES), LANES)
+        pair = [req_ref[s, rows_of, :], req_ref[s + 1, rows_of, :]]
+        cell = jnp.concatenate([r[0:1] for r in pair], axis=1).astype(I32)
+        hit = ones_where(iota((width, 2 * LANES), 0) == cell)
         corner_ref[...] = jnp.dot(table_ref[...], hit, preferred_element_type=F32)
-        cx = [corner_ref[n * rows : n * rows + members, :] for n in range(4)]
-        cy = [corner_ref[n * rows + members : (n + 1) * rows, :] for n in range(4)]
-        x = jnp.broadcast_to(r[1:2], (members, LANES))
-        y = jnp.broadcast_to(r[2:3], (members, LANES))
-        for _ in range(2):
-            mx = x + 0.5 * STEP * bilinear(cx, x, y)
-            my = y + 0.5 * STEP * bilinear(cy, x, y)
-            x = x + STEP * bilinear(cx, mx, my)
-            y = y + STEP * bilinear(cy, mx, my)
-        lanes = pl.ds(pl.multiple_of(b * LANES, LANES), LANES)
-        pred_ref[s, 0:members, lanes] = x
-        pred_ref[s, members:rows, lanes] = y
-        valid = r[6:7] > 0.5
-        deviation = jnp.where(valid, r[5:6], 1.0)
-        scale = jnp.where(valid, 1.0 / (deviation * spread), 0.0)
-        inverse = jnp.where(valid, 1.0 / deviation, 0.0)
-        mean_x = jnp.sum(x, axis=0, keepdims=True) * (1.0 / members)
-        mean_y = jnp.sum(y, axis=0, keepdims=True) * (1.0 / members)
-        anomaly = jnp.concatenate([(x - mean_x) * scale, (y - mean_y) * scale], axis=1)
-        innovation = jnp.concatenate([(r[3:4] - mean_x) * inverse, (r[4:5] - mean_y) * inverse], axis=1)
-        first = iota((8, 2 * LANES), 0) == 0
-        both = jnp.concatenate([anomaly, jnp.where(first, innovation, 0.0)], axis=0)
-        gram_ref[:, 0 : members + 8] += lax.dot_general(anomaly, both, NT, precision=HIGHEST, preferred_element_type=F32)
-
-    def one_source(s, carry):
-        amount = block_count(req_ref[s, 7:8, :])
-        lax.fori_loop(0, amount, lambda b, c: (one_block(s, b), c)[1], 0)
+        both = []
+        for h, r in enumerate(pair):
+            half = slice(h * LANES, (h + 1) * LANES)
+            cx = [corner_ref[n * rows : n * rows + members, half] for n in range(4)]
+            cy = [corner_ref[n * rows + members : (n + 1) * rows, half] for n in range(4)]
+            x = jnp.broadcast_to(r[1:2], (members, LANES))
+            y = jnp.broadcast_to(r[2:3], (members, LANES))
+            for _ in range(2):
+                mx = x + 0.5 * STEP * bilinear(cx, x, y)
+                my = y + 0.5 * STEP * bilinear(cy, x, y)
+                x, y = x + STEP * bilinear(cx, mx, my), y + STEP * bilinear(cy, mx, my)
+            pred_ref[s + h, 0:members, lanes] = x
+            pred_ref[s + h, members:rows, lanes] = y
+            valid = r[6:7] > 0.5
+            deviation = jnp.where(valid, r[5:6], 1.0)
+            scale = jnp.where(valid, 1.0 / (deviation * spread), 0.0)
+            inverse = jnp.where(valid, 1.0 / deviation, 0.0)
+            for values, seen in ((x, r[3:4]), (y, r[4:5])):
+                mean = jnp.sum(values, axis=0, keepdims=True) * (1.0 / members)
+                first = iota((8, LANES), 0) == 0
+                last = jnp.where(first, (seen - mean) * inverse, 0.0)
+                both.append(jnp.concatenate([(values - mean) * scale, last], axis=0))
+        both = jnp.concatenate(both, axis=1)
+        gram_ref[:, 0 : members + 8] += lax.dot_general(
+            both[:members], both, NT, precision=HIGHEST, preferred_element_type=F32
+        )
+
+    def one_pair(n, carry):
+        amount = jnp.maximum(block_count(req_ref[2 * n, 7:8, :]), block_count(req_ref[2 * n + 1, 7:8, :]))
+        lax.fori_loop(0, amount, lambda b, c: (one_block(2 * n, b), c)[1], 0)
         return carry
 
-    lax.fori_loop(0, sources, one_source, 0)
+    lax.fori_loop(0, sources // 2, one_pair, 0)
 
 
 def observe(z, zero, requests, members, local):
@@ -218,41 +224,69 @@
             jax.ShapeDtypeStruct((sources, rows, per // 8 * LANES), F32),
             jax.ShapeDtypeStruct((members, LANES), F32),
         ],
-        scratch_shapes=[pltpu.VMEM((4 * rows, width), BF16), pltpu.VMEM((4 * rows, LANES), F32)],
+        scratch_shapes=[pltpu.VMEM((4 * rows, width), BF16), pltpu.VMEM((4 * rows, 2 * LANES), F32)],
         name="observe",
     )(z, requests, *zero)
 
 
-def all_sum(x):
+def all_sum_parts(x):
+    parts = [x]
     for axis in ("tile", "mem"):
         size = lax.axis_size(axis)
         bit = 1
         while bit < size:
-            if size // bit >= 4 and not (axis == "tile" and bit == 1):
-                a, b, c = [lax.ppermute(x, axis, [(n, n ^ (bit * k)) for n in range(size)]) for k in (1, 2, 3)]
-                x = (x + a) + (b + c)
-                bit *= 4
-            else:
-                x = x + lax.ppermute(x, axis, [(n, n ^ bit) for n in range(size)])
-                bit *= 2
-    return x
-
-
-def ensemble_weights(gram_matrix, projection):
-    members = gram_matrix.shape[0]
-    identity = jnp.eye(members, dtype=F32)
-    factor = jnp.linalg.cholesky(identity + gram_matrix)
-    half_solve = lax.linalg.triangular_solve(factor, projection[:, None], left_side=True, lower=True)
-    mean_weight = lax.linalg.triangular_solve(factor, half_solve, left_side=True, lower=True, transpose_a=True)
-    inverse_root = lax.linalg.triangular_solve(factor, identity, left_side=True, lower=True, transpose_a=True)
-    combined = mean_weight + jnp.sqrt(F32(members - 1)) * inverse_root
-    return combined - jnp.mean(combined, axis=0, keepdims=True) + 1.0 / members
-
-
-def spread_kernel(members, local, levels, gap, z_ref, w_ref, mix0_ref, mix1_ref, pos_ref):
+            x = parts[0] if len(parts) == 1 else add_parts(parts)
+            many = 4 if size // bit >= 4 and not (axis == "tile" and bit == 1) else 2
+            parts = [x] + [swap(x, axis, bit * k) for k in range(1, many)]
+            bit *= many
+    return parts
+
+
+def add_parts(parts):
+    while len(parts) > 1:
+        parts = [a + b for a, b in zip(parts[0::2], parts[1::2])]
+    return parts[0]
+
+
+def eliminate(matrix):
+    members, lanes = matrix.shape
+    tiles = [matrix[n : n + 8] for n in range(0, members, 8)]
+    pivots = [jnp.ones((8, lanes), F32) for _ in tiles]
+    sub = iota((8, lanes), 0)
+    lane = iota((8, lanes), 1)
+    for j in range(members):
+        at, inside = j // 8, j % 8
+        source = tiles[at][inside : inside + 1]
+        pivot = jnp.broadcast_to(source[:, j : j + 1], (8, lanes))
+        row = jnp.where(lane == j, 1.0, jnp.broadcast_to(source, (8, lanes)))
+        scaled = row * (1.0 / pivot)
+        for n in range(at, len(tiles)):
+            factor = jnp.broadcast_to(tiles[n][:, j : j + 1], (8, lanes))
+            new = jnp.where(lane == j, 0.0, tiles[n]) - factor * scaled
+            if n == at:
+                new = jnp.where(sub > inside, new, jnp.where(sub == inside, row, tiles[n]))
+            tiles[n] = new
+        pivots[at] = jnp.where(sub == inside, pivot, pivots[at])
+    return jnp.concatenate(tiles, axis=0), jnp.concatenate(pivots, axis=0)
+
+
+def ensemble_weights(gram):
+    members, lanes = gram.shape
+    i = iota((members, lanes), 0)
+    j = iota((members, lanes), 1)
+    lower, pivots = eliminate(gram + jnp.where(i == j, 1.0, 0.0))
+    half = lower * lax.rsqrt(pivots)
+    inverse = jnp.where(j <= i, half, 0.0)[:, :members]
+    mean = lax.dot_general(half, inverse, TN, precision=HIGHEST, preferred_element_type=F32)[members : members + 1]
+    combined = mean + math.sqrt(members - 1) * inverse
+    return combined - jnp.mean(combined, axis=1, keepdims=True) + 1.0 / members
+
+
+def spread_kernel(members, local, levels, gap, z_ref, *refs):
+    gram_refs, (mix0_ref, mix1_ref, pos_ref) = refs[:-3], refs[-3:]
     z = z_ref[0]
     other = levels - 1
-    weights = w_ref[...]
+    weights = ensemble_weights(add_parts([ref[...] for ref in gram_refs]))
 
     def member_of(index, each):
         r = quotient(index, local * each)
@@ -262,7 +296,7 @@
     rows = members * levels
     i = iota((rows, members), 0)
     repeat = ones_where(member_of(i, levels) == iota((rows, members), 1))
-    tall = lax.dot_general(repeat, weights.astype(BF16), NT, preferred_element_type=F32).astype(BF16)
+    tall = jnp.dot(repeat, weights.astype(BF16), preferred_element_type=F32).astype(BF16)
     shares, _, cols = mix0_ref.shape
     i = iota((rows, cols), 0)
     j = iota((rows, cols), 1)
@@ -282,7 +316,7 @@
             ref[s] = jnp.where(jnp.logical_or(same, zero), wide, 0.0).astype(BF16)
     i = iota((2 * members, members), 0)
     repeat = ones_where(member_of(i, 2) == iota((2 * members, members), 1), F32)
-    tall = lax.dot_general(repeat, weights, NT, precision=HIGHEST, preferred_element_type=F32)
+    tall = jnp.dot(repeat, weights, precision=HIGHEST, preferred_element_type=F32)
     odd = i - 2 * quotient(i, 2) == 1
     pos_ref[:, :members] = jnp.where(odd, 0.0, tall)
     pos_ref[:, members:] = jnp.where(odd, tall, 0.0)
@@ -293,13 +327,13 @@
     return gap, round_up(gap + 2 * local, 16)
 
 
-def spread_weights(z, weights, local, levels):
-    members = weights.shape[0]
+def spread_weights(z, gram_parts, local, levels):
+    members = gram_parts[0].shape[0]
     rows = members * levels
     gap, cols = mix_sizes(local, levels)
     return pl.pallas_call(
         functools.partial(spread_kernel, members, local, levels, gap),
-        in_specs=[smem(), vmem()],
+        in_specs=[smem()] + [vmem()] * len(gram_parts),
         out_specs=[vmem()] * 3,
         out_shape=[
             jax.ShapeDtypeStruct((members // local, rows, cols), BF16),
@@ -307,7 +341,7 @@
             jax.ShapeDtypeStruct((2 * members, 2 * members), F32),
         ],
         name="spread",
-    )(z, weights)
+    )(z, *gram_parts)
 
 
 def mix_kernel(shares, gap, w_ref, *refs):
@@ -371,19 +405,22 @@
     sources, _, _ = pred_ref.shape
     out_ref[...] = jnp.zeros_like(out_ref)
 
-    def one_source(s, carry):
-        amount = block_count(req_ref[s, 7:8, :])
+    def one_pair(n, carry):
+        s = 2 * n
+        amount = jnp.maximum(block_count(req_ref[s, 7:8, :]), block_count(req_ref[s + 1, 7:8, :]))
 
         def one_block(b, c):
             lanes = pl.ds(pl.multiple_of(b * LANES, LANES), LANES)
-            moved = jnp.dot(w_ref[...], pred_ref[s, :, lanes], precision=HIGHEST, preferred_element_type=F32)
-            out_ref[s, :, lanes] = moved.astype(BF16)
+            both = jnp.concatenate([pred_ref[s, :, lanes], pred_ref[s + 1, :, lanes]], axis=1)
+            moved = jnp.dot(w_ref[...], both, precision=HIGHEST, preferred_element_type=F32).astype(BF16)
+            out_ref[s, :, lanes] = moved[:, :LANES]
+            out_ref[s + 1, :, lanes] = moved[:, LANES:]
             return c
 
         lax.fori_loop(0, amount, one_block, 0)
         return carry
 
-    lax.fori_loop(0, sources, one_source, 0)
+    lax.fori_loop(0, sources // 2, one_pair, 0)
 
 
 def move(pred, requests, w_pos):
@@ -448,10 +485,6 @@
     for r in range(1, len(pieces)):
         got.append(swap(pieces[r], axis, r))
     return got
-
-
-def after(pieces, other):
-    return lax.optimization_barrier((pieces, other))[0]
 
 
 def assimilate(velocity, start_frac, observed, obs_sd, tile_of, cell_of):
@@ -470,10 +503,8 @@
     requests = exchange(requests, "tile")
     rest0 = trade(rest0, "mem")
     pred, gram = observe(z, zero, requests, members, local)
-    gram = all_sum(gram)
-    rest1 = trade(after(rest1, gram), "mem")
-    weights = ensemble_weights(gram[:, :members], gram[:, members])
-    w_mix0, w_mix1, w_pos = spread_weights(z, weights, local, levels)
+    rest1 = trade(rest1, "mem")
+    w_mix0, w_mix1, w_pos = spread_weights(z, all_sum_parts(gram), local, levels)
 
     mixed0 = trade(mix(rest0, zero, w_mix0, local, levels), "mem")
     mixed1 = trade(mix(rest1, zero, w_mix1, local, levels), "mem")

time: 256 us -> 246 us (0.961)
  other arithmetic: 19.1 us -> 0.94 us
  Pallas kernels: 59 us -> 66.9 us
    another operation x5 -> x0, other arithmetic: 17.5 us -> none  [the longest x3 9.45 us: ensemble_weights(): factor = jnp.linalg.cholesky(identity + gram_matrix)]
    pallas_call x1, Pallas kernels: 3.47 us -> 16.7 us  [spread_weights(): pl.pallas_call(functools.partial(spread_kernel, members, local, levels, g...]
    ppermute x17 -> x24, starting transfers between devices: 34.5 us -> 47.3 us  [swap(): lax.ppermute(x, axis, [(n, n ^ bits) for n in range(lax.axis_size(axis))])]
    ppermute x7 -> x0, starting transfers between devices: 12.5 us -> none  [the longest x6 12.5 us: all_sum(): lax.ppermute(x, axis, [(n, n ^ bit * k) for n in range(size)])]
    ppermute x17 -> x24, waiting for transfers between devices: 105 us -> 113 us  [swap(): lax.ppermute(x, axis, [(n, n ^ bits) for n in range(lax.axis_size(axis))])]
    ppermute x7 -> x0, waiting for transfers between devices: 8.42 us -> none  [the longest x6 6.98 us: all_sum(): lax.ppermute(x, axis, [(n, n ^ bit * k) for n in range(size)])]
    pallas_call x1, Pallas kernels: 13.9 us -> 10.4 us  [observe(): pl.pallas_call(functools.partial(observe_kernel, members, local), in_spec...]
    unnamed x36 -> x46, local copies, waits for them, and re-layouts: 6.04 us -> 6.63 us
  transfers between devices with their start and end apart: 26 -> 26, of which waited for: 13 -> 13; matrix products, arithmetic and copies ran while one was open for 0% -> 0% of each run, Pallas kernels for 12% -> 13%
where the time goes in v2:
time: 246 us
  waiting for transfers between devices  113 us (46%)
  Pallas kernels  66.9 us (27%)
  starting transfers between devices  56.3 us (23%)
  local copies, waits for them, and re-layouts  7.62 us (3%)
    ppermute x24, waiting for transfers between devices, swap(): lax.ppermute(x, axis, [(n, n ^ bits) for n in range(lax.axis_size(axis))])  113 us
    ppermute x24, starting transfers between devices, swap(): lax.ppermute(x, axis, [(n, n ^ bits) for n in range(lax.axis_size(axis))])  47.3 us
    pallas_call x1, Pallas kernels, spread_weights(): pl.pallas_call(functools.partial(spread_kernel, members, local, levels, g...  16.7 us
    pallas_call x3, Pallas kernels, call(): pl.pallas_call(kernel, in_specs=[smem(), vmem()], out_specs=[vmem()] * sh...  10.5 us
    pallas_call x1, Pallas kernels, observe(): pl.pallas_call(functools.partial(observe_kernel, members, local), in_spec...  10.4 us
    all_to_all x2, starting transfers between devices, exchange(): return lax.all_to_all(x, axis, split_axis=0, concat_axis=0, tiled=True)  8.96 us
    pallas_call x2, Pallas kernels, mix(): pl.pallas_call(functools.partial(mix_kernel, shares, gap), in_specs=[vmem...  8.82 us
    pallas_call x1, Pallas kernels, settle(): pl.pallas_call(settle_kernel, in_specs=[vmem()] * 3, out_specs=[vmem()] *...  6.67 us
  transfers between devices with their start and end apart: 26, of which 13 were waited for; matrix products, arithmetic and copies ran while one was open for 0% of the time, Pallas kernels for 13%

profile of v2, /device:TPU:0, one launch (start us, length us, event | category | flops | bytes accessed | tf_op | source)
XLA Modules:
  0.0 245.6 jit_solution(18333131737136008579)
XLA Ops:
  0.6 3.6 %route.1 = (f32[8,32,128]{2,1,0:T(8,128)}, s32[1,2048]{1,0:T(1,128)}, f32[8,128]{1,0:T(8,128)}) custom-call(s32[1]{0:T(128)} %bitcast.q_ref.z_ref, s32[1,2048]{1,0:T(1,128)} %bitcast.24, s32[1,2048]{1,0:T(1,128)} %bitcast.25, f32[2,2048]{1,0:T(2,128)} %frac_ref.1, f32[2,2048]{1,0:T(2,128)} %obs_ref.1, f32[1,2048]{1,0:T(1,128)} %bitcast.26), custom_call_target="tpu_custom_call" | custom-call | tf_op jit(solution)/shard_map/route/pallas_call | solution.py:128
  4.2 5.2 %all-to-all-start = ((f32[8,32,128]{2,1,0:T(8,128)}), f32[8,32,128]{2,1,0:T(8,128)S(1)}, u32[]{:S(2)}, u32[]{:S(2)}) async-start(f32[8,32,128]{2,1,0:T(8,128)} %get-tuple-element.32), calls=%async_computation | async-start | bytes 262144 | tf_op jit(solution)/shard_map/all_to_all | solution.py:476
  9.4 3.3 %shard_map.77 = (bf16[48,1152]{1,0:T(8,128)(2,1)}, bf16[48,1152]{1,0:T(8,128)(2,1)}, bf16[48,1152]{1,0:T(8,128)(2,1)}, bf16[48,1152]{1,0:T(8,128)(2,1)}) custom-call(s32[1]{0:T(128)} %bitcast.q_ref.z_ref, bf16[384,4096]{1,0:T(8,128)(2,1)} %bitcast.13), custom_call_target="tpu_custom_call" | custom-call | tf_op jit(solution)/shard_map/pallas_call | solution.py:82
  12.7 1.6 collective-permute-start
  14.3 2.6 %collective-permute-start.1 = (bf16[48,1152]{1,0:T(8,128)(2,1)}, bf16[48,1152]{1,0:T(8,128)(2,1)S(1)}, u32[]{:S(2)}, u32[]{:S(2)}) collective-permute-start(bf16[48,1152]{1,0:T(8,128)(2,1)} %get-tuple-element.35), channel_id=1, source_target_pairs={{0,2},{1,3},{2,0},{3,1},{4,6},{5,7},{6,4},{7,5},{8,10},{9,11},{10,... | collective-permute-start | bytes 331784 | tf_op jit(solution)/shard_map/ppermute | solution.py:480
  16.9 0.2 collective-permute-start.2
  17.1 3.0 %collective-permute-done.refs_1_.refs_5_ = bf16[48,1152]{1,0:T(8,128)(2,1)S(1)} collective-permute-done((bf16[48,1152]{1,0:T(8,128)(2,1)}, bf16[48,1152]{1,0:T(8,128)(2,1)S(1)}, u32[]{:S(2)}, u32[]{:S(2)}) %collective-permute-start) | collective-permute-done | bytes 110624 | tf_op jit(solution)/shard_map/ppermute | solution.py:480
  20.1 6.0 %collective-permute-done.1.refs_2_.refs_6_ = bf16[48,1152]{1,0:T(8,128)(2,1)S(1)} collective-permute-done((bf16[48,1152]{1,0:T(8,128)(2,1)}, bf16[48,1152]{1,0:T(8,128)(2,1)S(1)}, u32[]{:S(2)}, u32[]{:S(2)}) %collective-permute-start.1) | collective-permute-done | bytes 110624 | tf_op jit(solution)/shard_map/ppermute | solution.py:480
  26.1 0.0 all-to-all-done.req_ref
  26.2 0.6 copy-done.3
  26.8 0.0 copy-done.4
  26.8 0.1 copy-done.1
  26.9 10.4 %observe.1 = (f32[8,192,512]{2,1,0:T(8,128)}, f32[96,128]{1,0:T(8,128)}) custom-call(s32[1]{0:T(128)} %bitcast.q_ref.z_ref, f32[8,32,128]{2,1,0:T(8,128)} %copy-done.1, bf16[48,1152]{1,0:T(8,128)(2,1)} %get-tuple-element.33.refs_0_.refs_4_, bf16[48,1152]{1,0:T(8,128)(2,1)} %copy-done.2, bf16[48,1152]{1,0:T(8,128)(2,1)} %copy-done.3, bf16[48,1152]{1,0:T(8,128)(2,1)} %copy-done.4), custom_call_target="tpu_custom_call" | custom-call | tf_op jit(solution)/shard_map/observe/pallas_call | solution.py:219
  37.3 0.0 collective-permute-start.3
  37.3 1.4 collective-permute-done.3
  38.7 0.8 add.18
  39.5 5.8 %collective-permute-start.4 = (f32[96,128]{1,0:T(8,128)S(1)}, f32[96,128]{1,0:T(8,128)S(1)}, u32[]{:S(2)}, u32[]{:S(2)}) collective-permute-start(f32[96,128]{1,0:T(8,128)S(1)} %add.18), channel_id=1, source_target_pairs={{0,8},{4,12},{8,0},{12,4},{16,24},{20,28},{24,16},{28,20},{1,9},{5... | collective-permute-start | bytes 147464 | tf_op jit(solution)/shard_map/ppermute | solution.py:480
  45.3 0.0 collective-permute-start.5
  45.3 1.5 collective-permute-start.6
  46.8 0.7 collective-permute-done.4
  47.6 2.9 %collective-permute-done.5 = f32[96,128]{1,0:T(8,128)S(1)} collective-permute-done((f32[96,128]{1,0:T(8,128)S(1)}, f32[96,128]{1,0:T(8,128)S(1)}, u32[]{:S(2)}, u32[]{:S(2)}) %collective-permute-start.5) | collective-permute-done | bytes 49184 | tf_op jit(solution)/shard_map/ppermute | solution.py:480
  50.5 2.9 %collective-permute-start.7 = (f32[96,128]{1,0:T(8,128)S(1)}, f32[96,128]{1,0:T(8,128)S(1)}, u32[]{:S(2)}, u32[]{:S(2)}) collective-permute-start(f32[96,128]{1,0:T(8,128)S(1)} %add_add_fusion.refs_0_), channel_id=1, source_target_pairs={{0,1},{1,0},{2,3},{3,2},{4,5},{5,4},{6,7},{7,6},{8,9},{9,8},{10,11... | collective-permute-start | bytes 147464 | tf_op jit(solution)/shard_map/ppermute | solution.py:480
  53.4 2.4 collective-permute-start.9
  55.9 2.6 %collective-permute-done.8.refs_2_ = f32[96,128]{1,0:T(8,128)S(1)} collective-permute-done((f32[96,128]{1,0:T(8,128)S(1)}, f32[96,128]{1,0:T(8,128)S(1)}, u32[]{:S(2)}, u32[]{:S(2)}) %collective-permute-start.8) | collective-permute-done | bytes 49184 | tf_op jit(solution)/shard_map/ppermute | solution.py:480
  58.5 1.0 collective-permute-done.9.refs_3_
  59.4 0.6 copy-done.21
  60.0 16.7 %spread.1 = (bf16[4,768,224]{2,1,0:T(8,128)(2,1)}, bf16[4,768,224]{2,1,0:T(8,128)(2,1)}, f32[192,192]{1,0:T(8,128)}) custom-call(s32[1]{0:T(128)} %bitcast.q_ref.z_ref, f32[96,128]{1,0:T(8,128)} %copy-done.18, f32[96,128]{1,0:T(8,128)} %copy-done.19, f32[96,128]{1,0:T(8,128)} %copy-done.20, f32[96,128]{1,0:T(8,128)} %copy-done.21), custom_call_target="tpu_custom_call" | custom-call | tf_op jit(solution)/shard_map/spread/pallas_call | solution.py:334
  76.7 5.1 %move.1 = bf16[8,192,512]{2,1,0:T(8,128)(2,1)} custom-call(f32[8,192,512]{2,1,0:T(8,128)} %get-tuple-element.56.pred_ref, f32[8,32,128]{2,1,0:T(8,128)} %copy-done.1, f32[192,192]{1,0:T(8,128)} %get-tuple-element.57.w_ref), custom_call_target="tpu_custom_call" | custom-call | tf_op jit(solution)/shard_map/move/pallas_call | solution.py:427
  81.8 3.8 %all-to-all-start.1 = ((bf16[8,192,512]{2,1,0:T(8,128)(2,1)}), bf16[8,192,512]{2,1,0:T(8,128)(2,1)S(1)}, u32[]{:S(2)}, u32[]{:S(2)}) async-start(bf16[8,192,512]{2,1,0:T(8,128)(2,1)} %move.1), calls=%async_computation.1 | async-start | bytes 3145728 | tf_op jit(solution)/shard_map/all_to_all | solution.py:476
  85.5 3.6 %shard_map.79 = (bf16[168,1024]{1,0:T(8,128)(2,1)}, bf16[168,1024]{1,0:T(8,128)(2,1)}, bf16[168,1024]{1,0:T(8,128)(2,1)}, bf16[168,1024]{1,0:T(8,128)(2,1)}) custom-call(s32[1]{0:T(128)} %bitcast.q_ref.z_ref, bf16[384,4096]{1,0:T(8,128)(2,1)} %bitcast.14), custom_call_target="tpu_custom_call" | custom-call | tf_op jit(solution)/shard_map/pallas_call | solution.py:82
  89.1 0.7 collective-permute-start.16
  89.8 2.3 collective-permute-start.17
  92.1 1.4 collective-permute-start.18
  93.5 3.6 %shard_map.78 = (bf16[168,1024]{1,0:T(8,128)(2,1)}, bf16[168,1024]{1,0:T(8,128)(2,1)}, bf16[168,1024]{1,0:T(8,128)(2,1)}, bf16[168,1024]{1,0:T(8,128)(2,1)}) custom-call(s32[1]{0:T(128)} %bitcast.q_ref.z_ref, bf16[384,4096]{1,0:T(8,128)(2,1)} %bitcast.15), custom_call_target="tpu_custom_call" | custom-call | tf_op jit(solution)/shard_map/pallas_call | solution.py:82
  97.1 9.9 %collective-permute-done.16.refs_1_ = bf16[168,1024]{1,0:T(8,128)(2,1)S(1)} collective-permute-done((bf16[168,1024]{1,0:T(8,128)(2,1)}, bf16[168,1024]{1,0:T(8,128)(2,1)S(1)}, u32[]{:S(2)}, u32[]{:S(2)}) %collective-permute-start.16) | collective-permute-done | bytes 344096 | tf_op jit(solution)/shard_map/ppermute | solution.py:480
  107.0 9.6 %collective-permute-done.17.refs_2_ = bf16[168,1024]{1,0:T(8,128)(2,1)S(1)} collective-permute-done((bf16[168,1024]{1,0:T(8,128)(2,1)}, bf16[168,1024]{1,0:T(8,128)(2,1)S(1)}, u32[]{:S(2)}, u32[]{:S(2)}) %collective-permute-start.17) | collective-permute-done | bytes 344096 | tf_op jit(solution)/shard_map/ppermute | solution.py:480
  116.6 0.7 copy-done.16
  117.4 0.2 copy-done.17
  117.5 4.4 %mix.3 = (bf16[192,1024]{1,0:T(8,128)(2,1)}, bf16[192,1024]{1,0:T(8,128)(2,1)}, bf16[192,1024]{1,0:T(8,128)(2,1)}, bf16[192,1024]{1,0:T(8,128)(2,1)}) custom-call(bf16[4,768,224]{2,1,0:T(8,128)(2,1)} %get-tuple-element.47.w_ref, bf16[168,1024]{1,0:T(8,128)(2,1)} %get-tuple-element.48.refs_0_, bf16[168,1024]{1,0:T(8,128)(2,1)} %copy-done.14, ...), custom_call_target="tpu_custom_call" | custom-call | tf_op jit(solution)/shard_map/mix/pallas_call | solution.py:367
  122.0 6.8 %collective-permute-start.19 = (bf16[192,1024]{1,0:T(8,128)(2,1)}, bf16[192,1024]{1,0:T(8,128)(2,1)S(1)}, u32[]{:S(2)}, u32[]{:S(2)}) collective-permute-start(bf16[192,1024]{1,0:T(8,128)(2,1)} %get-tuple-element.53), channel_id=1, source_target_pairs={{0,1},{1,0},{2,3},{3,2},{4,5},{5,4},{6,7},{7,6},{8,9},{9,8},{10,11... | collective-permute-start | bytes 1179656 | tf_op jit(solution)/shard_map/ppermute | solution.py:480
  128.8 1.1 copy-done
  129.9 6.7 %settle.1 = (bf16[2,48,2048]{2,1,0:T(8,128)(2,1)}, bf16[2,48,2048]{2,1,0:T(8,128)(2,1)}) custom-call(bf16[8,192,512]{2,1,0:T(8,128)(2,1)} %copy-done, s32[1,2048]{1,0:T(1,128)} %get-tuple-element.58.where_ref, f32[8,128]{1,0:T(8,128)} %get-tuple-element.59.count_ref), custom_call_target="tpu_custom_call" | custom-call | tf_op jit(solution)/shard_map/settle/pallas_call | solution.py:465
  136.6 2.9 %collective-permute-start.11 = (bf16[168,1024]{1,0:T(8,128)(2,1)}, bf16[168,1024]{1,0:T(8,128)(2,1)S(1)}, u32[]{:S(2)}, u32[]{:S(2)}) collective-permute-start(bf16[168,1024]{1,0:T(8,128)(2,1)} %get-tuple-element.41), channel_id=1, source_target_pairs={{0,2},{1,3},{2,0},{3,1},{4,6},{5,7},{6,4},{7,5},{8,10},{9,11},{10,... | collective-permute-start | bytes 1032200 | tf_op jit(solution)/shard_map/ppermute | solution.py:480
  139.5 1.5 collective-permute-start.12
  141.0 0.7 copy-done.12
  141.7 0.0 collective-permute-start.20
  141.7 34.3 %collective-permute-done.11.refs_2_ = bf16[168,1024]{1,0:T(8,128)(2,1)S(1)} collective-permute-done((bf16[168,1024]{1,0:T(8,128)(2,1)}, bf16[168,1024]{1,0:T(8,128)(2,1)S(1)}, u32[]{:S(2)}, u32[]{:S(2)}) %collective-permute-start.11) | collective-permute-done | bytes 344096 | tf_op jit(solution)/shard_map/ppermute | solution.py:480
  176.0 2.4 collective-permute-start.21
  178.4 0.8 copy-done.15
  179.2 4.4 %mix.2 = (bf16[192,1024]{1,0:T(8,128)(2,1)}, bf16[192,1024]{1,0:T(8,128)(2,1)}, bf16[192,1024]{1,0:T(8,128)(2,1)}, bf16[192,1024]{1,0:T(8,128)(2,1)}) custom-call(bf16[4,768,224]{2,1,0:T(8,128)(2,1)} %get-tuple-element.38.w_ref, bf16[168,1024]{1,0:T(8,128)(2,1)} %get-tuple-element.39.refs_0_, bf16[168,1024]{1,0:T(8,128)(2,1)} %copy-done.12, ...), custom_call_target="tpu_custom_call" | custom-call | tf_op jit(solution)/shard_map/mix/pallas_call | solution.py:367
  183.6 9.8 %collective-permute-start.13 = (bf16[192,1024]{1,0:T(8,128)(2,1)}, bf16[192,1024]{1,0:T(8,128)(2,1)S(1)}, u32[]{:S(2)}, u32[]{:S(2)}) collective-permute-start(bf16[192,1024]{1,0:T(8,128)(2,1)} %get-tuple-element.44), channel_id=1, source_target_pairs={{0,1},{1,0},{2,3},{3,2},{4,5},{5,4},{6,7},{7,6},{8,9},{9,8},{10,11... | collective-permute-start | bytes 1179656 | tf_op jit(solution)/shard_map/ppermute | solution.py:480
  193.4 1.0 collective-permute-start.14
  194.3 1.5 collective-permute-start.15
  195.8 0.1 add.22
  195.9 8.8 %collective-permute-done.20 = bf16[192,1024]{1,0:T(8,128)(2,1)S(1)} collective-permute-done((bf16[192,1024]{1,0:T(8,128)(2,1)}, bf16[192,1024]{1,0:T(8,128)(2,1)S(1)}, u32[]{:S(2)}, u32[]{:S(2)}) %collective-permute-start.20) | collective-permute-done | bytes 393248 | tf_op jit(solution)/shard_map/ppermute | solution.py:480
  204.8 0.7 copy-done.9
  205.5 0.1 copy-done.10
  205.6 2.6 %join.2.refs_4_ = bf16[24,2,8,4096]{3,2,1,0:T(8,128)(2,1)} custom-call(s32[1]{0:T(128)} %bitcast.q_ref.z_ref, bf16[24,8,1024]{2,1,0:T(8,128)(2,1)} %bitcast.20, bf16[24,8,1024]{2,1,0:T(8,128)(2,1)} %bitcast.21, bf16[24,8,1024]{2,1,0:T(8,128)(2,1)} %bitcast.22, bf16[24,8,1024]{2,1,0:T(8,128)(2,1)} %bitcast.23), custom_call_target="tpu_custom_call" | custom-call | tf_op jit(solution)/shard_map/join/pallas_call | solution.py:391
  208.2 25.8 %collective-permute-done.14 = bf16[192,1024]{1,0:T(8,128)(2,1)S(1)} collective-permute-done((bf16[192,1024]{1,0:T(8,128)(2,1)}, bf16[192,1024]{1,0:T(8,128)(2,1)S(1)}, u32[]{:S(2)}, u32[]{:S(2)}) %collective-permute-start.14) | collective-permute-done | bytes 393248 | tf_op jit(solution)/shard_map/ppermute | solution.py:480
  234.0 0.8 copy-done.6
  234.8 0.1 copy-done.7
  234.9 2.6 %join.3 = bf16[24,2,8,4096]{3,2,1,0:T(8,128)(2,1)} custom-call(s32[1]{0:T(128)} %bitcast.q_ref.z_ref, bf16[24,8,1024]{2,1,0:T(8,128)(2,1)} %bitcast.16, bf16[24,8,1024]{2,1,0:T(8,128)(2,1)} %bitcast.17, bf16[24,8,1024]{2,1,0:T(8,128)(2,1)} %bitcast.18, bf16[24,8,1024]{2,1,0:T(8,128)(2,1)} %bitcast.19, ...), custom_call_target="tpu_custom_call", output_to_operand_aliasing={{}: (5, {})} | custom-call | tf_op jit(solution)/shard_map/join/pallas_call | solution.py:391
  237.5 7.1 %collective-permute-done.23 = bf16[1,48,2048]{2,1,0:T(8,128)(2,1)S(1)} collective-permute-done((bf16[1,48,2048]{2,1,0:T(8,128)(2,1)S(1)}, bf16[1,48,2048]{2,1,0:T(8,128)(2,1)S(1)}, u32[]{:S(2)}, u32[]{:S(2)}) %collective-permute-start.23) | collective-permute-done | bytes 196640 | tf_op jit(solution)/shard_map/ppermute | solution.py:480
  244.6 1.0 reshape.60
  (52 shorter events, 0.2 us)
Async XLA Ops:
  4.2 21.9 %all-to-all-start = ((f32[8,32,128]{2,1,0:T(8,128)}), f32[8,32,128]{2,1,0:T(8,128)S(1)}, u32[]{:S(2)}, u32[]{:S(2)}) async-start(f32[8,32,128]{2,1,0:T(8,128)} %get-tuple-element.32), calls=%async_computation | async-start | bytes 262144 | tf_op jit(solution)/shard_map/all_to_all | solution.py:476
  12.7 7.4 %collective-permute-start = (bf16[48,1152]{1,0:T(8,128)(2,1)}, bf16[48,1152]{1,0:T(8,128)(2,1)S(1)}, u32[]{:S(2)}, u32[]{:S(2)}) collective-permute-start(bf16[48,1152]{1,0:T(8,128)(2,1)} %get-tuple-element.34), channel_id=1, source_target_pairs={{0,1},{1,0},{2,3},{3,2},{4,5},{5,4},{6,7},{7,6},{8,9},{9,8},{10,11... | collective-permute-start | bytes 331784 | tf_op jit(solution)/shard_map/ppermute | solution.py:480
  14.3 11.8 %collective-permute-start.1 = (bf16[48,1152]{1,0:T(8,128)(2,1)}, bf16[48,1152]{1,0:T(8,128)(2,1)S(1)}, u32[]{:S(2)}, u32[]{:S(2)}) collective-permute-start(bf16[48,1152]{1,0:T(8,128)(2,1)} %get-tuple-element.35), channel_id=1, source_target_pairs={{0,2},{1,3},{2,0},{3,1},{4,6},{5,7},{6,4},{7,5},{8,10},{9,11},{10,... | collective-permute-start | bytes 331784 | tf_op jit(solution)/shard_map/ppermute | solution.py:480
  16.9 9.2 %collective-permute-start.2 = (bf16[48,1152]{1,0:T(8,128)(2,1)}, bf16[48,1152]{1,0:T(8,128)(2,1)S(1)}, u32[]{:S(2)}, u32[]{:S(2)}) collective-permute-start(bf16[48,1152]{1,0:T(8,128)(2,1)} %get-tuple-element.36), channel_id=1, source_target_pairs={{0,3},{1,2},{2,1},{3,0},{4,7},{5,6},{6,5},{7,4},{8,11},{9,10},{10,... | collective-permute-start | bytes 331784 | tf_op jit(solution)/shard_map/ppermute | solution.py:480
  20.1 6.1 %copy-start.2 = (bf16[48,1152]{1,0:T(8,128)(2,1)}, bf16[48,1152]{1,0:T(8,128)(2,1)S(1)}, u32[]{:S(2)}) copy-start(bf16[48,1152]{1,0:T(8,128)(2,1)S(1)} %collective-permute-done.refs_1_.refs_5_) | copy-start | bytes 331780
  26.1 0.6 copy-start.3
  26.1 0.7 copy-start.4
  26.1 0.7 copy-start.1
  37.3 1.4 collective-permute-start.3
  39.5 8.0 %collective-permute-start.4 = (f32[96,128]{1,0:T(8,128)S(1)}, f32[96,128]{1,0:T(8,128)S(1)}, u32[]{:S(2)}, u32[]{:S(2)}) collective-permute-start(f32[96,128]{1,0:T(8,128)S(1)} %add.18), channel_id=1, source_target_pairs={{0,8},{4,12},{8,0},{12,4},{16,24},{20,28},{24,16},{28,20},{1,9},{5... | collective-permute-start | bytes 147464 | tf_op jit(solution)/shard_map/ppermute | solution.py:480
  45.3 5.1 %collective-permute-start.5 = (f32[96,128]{1,0:T(8,128)S(1)}, f32[96,128]{1,0:T(8,128)S(1)}, u32[]{:S(2)}, u32[]{:S(2)}) collective-permute-start(f32[96,128]{1,0:T(8,128)S(1)} %add.18), channel_id=1, source_target_pairs={{0,16},{4,20},{8,24},{12,28},{16,0},{20,4},{24,8},{28,12},{1,17},{... | collective-permute-start | bytes 147464 | tf_op jit(solution)/shard_map/ppermute | solution.py:480
  45.3 5.1 %collective-permute-start.6 = (f32[96,128]{1,0:T(8,128)S(1)}, f32[96,128]{1,0:T(8,128)S(1)}, u32[]{:S(2)}, u32[]{:S(2)}) collective-permute-start(f32[96,128]{1,0:T(8,128)S(1)} %add.18), channel_id=1, source_target_pairs={{0,24},{4,28},{8,16},{12,20},{16,8},{20,12},{24,0},{28,4},{1,25},{... | collective-permute-start | bytes 147464 | tf_op jit(solution)/shard_map/ppermute | solution.py:480
  50.5 8.9 %copy-start.18 = (f32[96,128]{1,0:T(8,128)}, f32[96,128]{1,0:T(8,128)S(1)}, u32[]{:S(2)}) copy-start(f32[96,128]{1,0:T(8,128)S(1)} %add_add_fusion.refs_0_) | copy-start | bytes 147460
  50.5 5.4 %collective-permute-start.7 = (f32[96,128]{1,0:T(8,128)S(1)}, f32[96,128]{1,0:T(8,128)S(1)}, u32[]{:S(2)}, u32[]{:S(2)}) collective-permute-start(f32[96,128]{1,0:T(8,128)S(1)} %add_add_fusion.refs_0_), channel_id=1, source_target_pairs={{0,1},{1,0},{2,3},{3,2},{4,5},{5,4},{6,7},{7,6},{8,9},{9,8},{10,11... | collective-permute-start | bytes 147464 | tf_op jit(solution)/shard_map/ppermute | solution.py:480
  53.4 5.0 %collective-permute-start.8 = (f32[96,128]{1,0:T(8,128)S(1)}, f32[96,128]{1,0:T(8,128)S(1)}, u32[]{:S(2)}, u32[]{:S(2)}) collective-permute-start(f32[96,128]{1,0:T(8,128)S(1)} %add_add_fusion.refs_0_), channel_id=1, source_target_pairs={{0,2},{1,3},{2,0},{3,1},{4,6},{5,7},{6,4},{7,5},{8,10},{9,11},{10,... | collective-permute-start | bytes 147464 | tf_op jit(solution)/shard_map/ppermute | solution.py:480
  53.4 6.0 %collective-permute-start.9 = (f32[96,128]{1,0:T(8,128)S(1)}, f32[96,128]{1,0:T(8,128)S(1)}, u32[]{:S(2)}, u32[]{:S(2)}) collective-permute-start(f32[96,128]{1,0:T(8,128)S(1)} %add_add_fusion.refs_0_), channel_id=1, source_target_pairs={{0,3},{1,2},{2,1},{3,0},{4,7},{5,6},{6,5},{7,4},{8,11},{9,10},{10,... | collective-permute-start | bytes 147464 | tf_op jit(solution)/shard_map/ppermute | solution.py:480
  55.9 3.6 %copy-start.19 = (f32[96,128]{1,0:T(8,128)}, f32[96,128]{1,0:T(8,128)S(1)}, u32[]{:S(2)}) copy-start(f32[96,128]{1,0:T(8,128)S(1)} %collective-permute-done.7.refs_1_) | copy-start | bytes 147460
  58.5 1.0 copy-start.20
  59.4 0.6 copy-start.21
  81.8 47.0 %all-to-all-start.1 = ((bf16[8,192,512]{2,1,0:T(8,128)(2,1)}), bf16[8,192,512]{2,1,0:T(8,128)(2,1)S(1)}, u32[]{:S(2)}, u32[]{:S(2)}) async-start(bf16[8,192,512]{2,1,0:T(8,128)(2,1)} %move.1), calls=%async_computation.1 | async-start | bytes 3145728 | tf_op jit(solution)/shard_map/all_to_all | solution.py:476
  89.1 17.9 %collective-permute-start.16 = (bf16[168,1024]{1,0:T(8,128)(2,1)}, bf16[168,1024]{1,0:T(8,128)(2,1)S(1)}, u32[]{:S(2)}, u32[]{:S(2)}) collective-permute-start(bf16[168,1024]{1,0:T(8,128)(2,1)} %get-tuple-element.49), channel_id=1, source_target_pairs={{0,1},{1,0},{2,3},{3,2},{4,5},{5,4},{6,7},{7,6},{8,9},{9,8},{10,11... | collective-permute-start | bytes 1032200 | tf_op jit(solution)/shard_map/ppermute | solution.py:480
  89.8 26.8 %collective-permute-start.17 = (bf16[168,1024]{1,0:T(8,128)(2,1)}, bf16[168,1024]{1,0:T(8,128)(2,1)S(1)}, u32[]{:S(2)}, u32[]{:S(2)}) collective-permute-start(bf16[168,1024]{1,0:T(8,128)(2,1)} %get-tuple-element.50), channel_id=1, source_target_pairs={{0,2},{1,3},{2,0},{3,1},{4,6},{5,7},{6,4},{7,5},{8,10},{9,11},{10,... | collective-permute-start | bytes 1032200 | tf_op jit(solution)/shard_map/ppermute | solution.py:480
  92.1 24.5 %collective-permute-start.18 = (bf16[168,1024]{1,0:T(8,128)(2,1)}, bf16[168,1024]{1,0:T(8,128)(2,1)S(1)}, u32[]{:S(2)}, u32[]{:S(2)}) collective-permute-start(bf16[168,1024]{1,0:T(8,128)(2,1)} %get-tuple-element.51), channel_id=1, source_target_pairs={{0,3},{1,2},{2,1},{3,0},{4,7},{5,6},{6,5},{7,4},{8,11},{9,10},{10,... | collective-permute-start | bytes 1032200 | tf_op jit(solution)/shard_map/ppermute | solution.py:480
  97.1 42.4 %copy-start.22 = (bf16[168,1024]{1,0:T(8,128)(2,1)S(1)}, bf16[168,1024]{1,0:T(8,128)(2,1)}, u32[]{:S(2)}) copy-start(bf16[168,1024]{1,0:T(8,128)(2,1)} %get-tuple-element.42) | copy-start | bytes 1032196
  97.1 43.9 %collective-permute-start.10 = (bf16[168,1024]{1,0:T(8,128)(2,1)}, bf16[168,1024]{1,0:T(8,128)(2,1)S(1)}, u32[]{:S(2)}, u32[]{:S(2)}) collective-permute-start(bf16[168,1024]{1,0:T(8,128)(2,1)} %get-tuple-element.40), channel_id=1, source_target_pairs={{0,1},{1,0},{2,3},{3,2},{4,5},{5,4},{6,7},{7,6},{8,9},{9,8},{10,11... | collective-permute-start | bytes 1032200 | tf_op jit(solution)/shard_map/ppermute | solution.py:480
  107.0 9.6 %copy-start.14 = (bf16[168,1024]{1,0:T(8,128)(2,1)}, bf16[168,1024]{1,0:T(8,128)(2,1)S(1)}, u32[]{:S(2)}) copy-start(bf16[168,1024]{1,0:T(8,128)(2,1)S(1)} %collective-permute-done.16.refs_1_) | copy-start | bytes 1032196
  116.6 0.7 copy-start.16
  116.6 0.9 copy-start.17
  122.0 71.4 %collective-permute-start.19 = (bf16[192,1024]{1,0:T(8,128)(2,1)}, bf16[192,1024]{1,0:T(8,128)(2,1)S(1)}, u32[]{:S(2)}, u32[]{:S(2)}) collective-permute-start(bf16[192,1024]{1,0:T(8,128)(2,1)} %get-tuple-element.53), channel_id=1, source_target_pairs={{0,1},{1,0},{2,3},{3,2},{4,5},{5,4},{6,7},{7,6},{8,9},{9,8},{10,11... | collective-permute-start | bytes 1179656 | tf_op jit(solution)/shard_map/ppermute | solution.py:480
  128.8 1.1 copy-start
  136.6 59.2 %copy-start.11 = (bf16[2,48,2048]{2,1,0:T(8,128)(2,1)S(1)}, bf16[2,48,2048]{2,1,0:T(8,128)(2,1)}, u32[]{:S(2)}) copy-start(bf16[2,48,2048]{2,1,0:T(8,128)(2,1)} %get-tuple-element.60) | copy-start | bytes 1179652
  136.6 57.8 %collective-permute-start.22 = (bf16[2,48,2048]{2,1,0:T(8,128)(2,1)}, bf16[2,48,2048]{2,1,0:T(8,128)(2,1)S(1)}, u32[]{:S(2)}, u32[]{:S(2)}) collective-permute-start(bf16[2,48,2048]{2,1,0:T(8,128)(2,1)} %get-tuple-element.61), channel_id=1, source_target_pairs={{0,1},{1,0},{2,3},{3,2},{4,5},{5,4},{6,7},{7,6},{8,9},{9,8},{10,11... | collective-permute-start | bytes 1179656 | tf_op jit(solution)/shard_map/ppermute | solution.py:480
  136.6 39.4 %collective-permute-start.11 = (bf16[168,1024]{1,0:T(8,128)(2,1)}, bf16[168,1024]{1,0:T(8,128)(2,1)S(1)}, u32[]{:S(2)}, u32[]{:S(2)}) collective-permute-start(bf16[168,1024]{1,0:T(8,128)(2,1)} %get-tuple-element.41), channel_id=1, source_target_pairs={{0,2},{1,3},{2,0},{3,1},{4,6},{5,7},{6,4},{7,5},{8,10},{9,11},{10,... | collective-permute-start | bytes 1032200 | tf_op jit(solution)/shard_map/ppermute | solution.py:480
  139.5 38.9 %collective-permute-start.12 = (bf16[168,1024]{1,0:T(8,128)(2,1)S(1)}, bf16[168,1024]{1,0:T(8,128)(2,1)S(1)}, u32[]{:S(2)}, u32[]{:S(2)}) collective-permute-start(bf16[168,1024]{1,0:T(8,128)(2,1)S(1)} %copy-done.22), channel_id=1, source_target_pairs={{0,3},{1,2},{2,1},{3,0},{4,7},{5,6},{6,5},{7,4},{8,11},{9,10},{10,... | collective-permute-start | bytes 1032200 | tf_op jit(solution)/shard_map/ppermute | solution.py:480
  141.0 0.7 copy-start.12
  141.7 63.0 %collective-permute-start.20 = (bf16[192,1024]{1,0:T(8,128)(2,1)}, bf16[192,1024]{1,0:T(8,128)(2,1)S(1)}, u32[]{:S(2)}, u32[]{:S(2)}) collective-permute-start(bf16[192,1024]{1,0:T(8,128)(2,1)} %get-tuple-element.54), channel_id=1, source_target_pairs={{0,2},{1,3},{2,0},{3,1},{4,6},{5,7},{6,4},{7,5},{8,10},{9,11},{10,... | collective-permute-start | bytes 1179656 | tf_op jit(solution)/shard_map/ppermute | solution.py:480
  176.0 2.4 copy-start.13
  176.0 28.7 %collective-permute-start.21 = (bf16[192,1024]{1,0:T(8,128)(2,1)}, bf16[192,1024]{1,0:T(8,128)(2,1)S(1)}, u32[]{:S(2)}, u32[]{:S(2)}) collective-permute-start(bf16[192,1024]{1,0:T(8,128)(2,1)} %get-tuple-element.55), channel_id=1, source_target_pairs={{0,3},{1,2},{2,1},{3,0},{4,7},{5,6},{6,5},{7,4},{8,11},{9,10},{10,... | collective-permute-start | bytes 1179656 | tf_op jit(solution)/shard_map/ppermute | solution.py:480
  178.4 0.8 copy-start.15
  183.6 24.6 %collective-permute-start.13 = (bf16[192,1024]{1,0:T(8,128)(2,1)}, bf16[192,1024]{1,0:T(8,128)(2,1)S(1)}, u32[]{:S(2)}, u32[]{:S(2)}) collective-permute-start(bf16[192,1024]{1,0:T(8,128)(2,1)} %get-tuple-element.44), channel_id=1, source_target_pairs={{0,1},{1,0},{2,3},{3,2},{4,5},{5,4},{6,7},{7,6},{8,9},{9,8},{10,11... | collective-permute-start | bytes 1179656 | tf_op jit(solution)/shard_map/ppermute | solution.py:480
  193.4 11.4 %copy-start.8 = (bf16[192,1024]{1,0:T(8,128)(2,1)}, bf16[192,1024]{1,0:T(8,128)(2,1)S(1)}, u32[]{:S(2)}) copy-start(bf16[192,1024]{1,0:T(8,128)(2,1)S(1)} %collective-permute-done.19) | copy-start | bytes 1179652
  193.4 40.6 %collective-permute-start.14 = (bf16[192,1024]{1,0:T(8,128)(2,1)}, bf16[192,1024]{1,0:T(8,128)(2,1)S(1)}, u32[]{:S(2)}, u32[]{:S(2)}) collective-permute-start(bf16[192,1024]{1,0:T(8,128)(2,1)} %get-tuple-element.45), channel_id=1, source_target_pairs={{0,2},{1,3},{2,0},{3,1},{4,6},{5,7},{6,4},{7,5},{8,10},{9,11},{10,... | collective-permute-start | bytes 1179656 | tf_op jit(solution)/shard_map/ppermute | solution.py:480
  194.3 39.7 %collective-permute-start.15 = (bf16[192,1024]{1,0:T(8,128)(2,1)}, bf16[192,1024]{1,0:T(8,128)(2,1)S(1)}, u32[]{:S(2)}, u32[]{:S(2)}) collective-permute-start(bf16[192,1024]{1,0:T(8,128)(2,1)} %get-tuple-element.46), channel_id=1, source_target_pairs={{0,3},{1,2},{2,1},{3,0},{4,7},{5,6},{6,5},{7,4},{8,11},{9,10},{10,... | collective-permute-start | bytes 1179656 | tf_op jit(solution)/shard_map/ppermute | solution.py:480
  204.7 0.8 copy-start.9
  204.7 39.8 %collective-permute-start.23 = (bf16[1,48,2048]{2,1,0:T(8,128)(2,1)S(1)}, bf16[1,48,2048]{2,1,0:T(8,128)(2,1)S(1)}, u32[]{:S(2)}, u32[]{:S(2)}) collective-permute-start(bf16[1,48,2048]{2,1,0:T(8,128)(2,1)S(1)} %slice.11), channel_id=1, source_target_pairs={{0,2},{1,3},{2,0},{3,1},{4,6},{5,7},{6,4},{7,5},{8,10},{9,11},{10,... | collective-permute-start | bytes 589832 | tf_op jit(solution)/shard_map/ppermute | solution.py:480
  204.8 0.9 copy-start.10
  208.2 25.8 %copy-start.5 = (bf16[192,1024]{1,0:T(8,128)(2,1)}, bf16[192,1024]{1,0:T(8,128)(2,1)S(1)}, u32[]{:S(2)}) copy-start(bf16[192,1024]{1,0:T(8,128)(2,1)S(1)} %collective-permute-done.13) | copy-start | bytes 1179652
  234.0 0.8 copy-start.6
  234.0 0.9 copy-start.7
